TPU v7x, 32 devices: a whole 2x2x4 slice. The times are simulated.
32 devices in a mesh: wide: 16 (over z, y, core), narrow: 2 (over x).
Axes of the slice: x: 2, y: 2, z: 4, core: 2. Of those that a mesh axis runs over, the one named last changes fastest.
Arguments:
- residual: bfloat16 [384, 5120], P(None, 'narrow'), may hold values from -70 to 70
- norm_gain: bfloat16 [5120], P('narrow'), may hold values from 0.5 to 1.5
- grad_out: bfloat16 [384, 5120], P(None, 'narrow'), may hold values from -6 to 6
- w_gate: bfloat16 [5120, 27648], P('narrow', 'wide'), may hold values from -0.078125 to 0.078125
- w_up: bfloat16 [5120, 27648], P('narrow', 'wide'), may hold values from -0.078125 to 0.078125
- w_down: bfloat16 [27648, 5120], P('wide', 'narrow'), may hold values from -0.0390625 to 0.0390625
- w_output: bfloat16 [5120, 5120], P('narrow', 'wide'), may hold values from -0.078125 to 0.078125
- query: bfloat16 [384, 5120], P('narrow'), may hold values from -6 to 6
- key: bfloat16 [384, 1024], P('narrow'), may hold values from -6 to 6
- value: bfloat16 [384, 1024], P('narrow'), may hold values from -6 to 6
- cache_key: bfloat16 [32768, 1024], P('wide', 'narrow'), may hold values from -10 to 10
- cache_value: bfloat16 [32768, 1024], P('wide', 'narrow'), may hold values from -6 to 6
- visible_from: int32 [384], replicated, may hold values from 0 to 16383
Outputs:
- grad_residual: bfloat16 [384, 5120], P(None, 'narrow')
- grad_gain: float32 [5120], P('narrow')
- grad_w_gate: bfloat16 [5120, 27648], P('narrow', 'wide')
- grad_w_up: bfloat16 [5120, 27648], P('narrow', 'wide')
- grad_w_down: bfloat16 [27648, 5120], P('wide', 'narrow')
- grad_w_output: bfloat16 [5120, 5120], P('narrow', 'wide')
- grad_query: bfloat16 [384, 5120], P(None, 'narrow')
All inputs are finite; a program needn't handle non-finite values.
Results may differ from a plain program's by a relative error of at most 0.01.
Values may be sent and summed in bfloat16 or wider, within the bound.
A program may use at most 320 MiB of HBM per device.

v0:
```python
import math

import jax
import jax.numpy as jnp
from jax import lax
from jax.sharding import PartitionSpec as P

D = 5120
HEAD_DIM = 128


EPSILON = 1e-06


def combined_all(array, axis, combine):
    everything = jax.tree.map(lambda part: lax.all_gather(part, axis), array)
    first = jax.tree.map(lambda part: part[0], everything)

    def hop(k, so_far):
        return combine(so_far, jax.tree.map(lambda part: part[k], everything))

    return lax.fori_loop(1, lax.axis_size(axis), hop, first)


def contract_rows(left, right):
    return lax.dot_general(
        left, right, (((0,), (0,)), ((), ())), preferred_element_type=jnp.float32
    )


def contract_cols(left, right):
    return lax.dot_general(
        left, right, (((1,), (1,)), ((), ())), preferred_element_type=jnp.float32
    )


def width_sum(parts):
    return lax.psum(parts, "narrow")


def wide_total(parts):
    return lax.psum(parts, "wide")


def merge_softmax(first, second):
    top = jnp.maximum(first[0], second[0])
    total = first[1] * jnp.exp(first[0] - top) + second[1] * jnp.exp(second[0] - top)
    return (top, total)


def swiglu_back(gate, up, hidden_grad):
    sigmoid_gate = jax.nn.sigmoid(gate)
    silu_gate = gate * sigmoid_gate
    activated = (silu_gate * up).astype(jnp.bfloat16)
    d_gate = (hidden_grad * up * sigmoid_gate * (1.0 + gate * (1.0 - sigmoid_gate))).astype(
        jnp.bfloat16
    )
    d_up = (hidden_grad * silu_gate).astype(jnp.bfloat16)
    return (activated, d_gate, d_up)


def to_groups(rows, groups):
    return rows.reshape(rows.shape[0], groups, HEAD_DIM).transpose(1, 0, 2)


def heads_grouped(rows, groups, per_group):
    return rows.reshape(rows.shape[0], groups, per_group, HEAD_DIM).transpose(1, 2, 0, 3)


def from_groups(block):
    return block.transpose(2, 0, 1, 3).reshape(block.shape[2], -1)


def per_device(
    residual,
    norm_gain,
    grad_out,
    w_gate,
    w_up,
    w_down,
    w_output,
    query,
    key,
    value,
    cache_key,
    cache_value,
    visible_from,
):
    wide_count = lax.axis_size("wide")
    wide_place = lax.axis_index("wide")
    tokens = residual.shape[0]
    scale = 1.0 / math.sqrt(HEAD_DIM)
    queries, stretch_keys, stretch_values = (
        lax.all_to_all(query, "narrow", split_axis=1, concat_axis=0, tiled=True),
        lax.all_to_all(key, "narrow", split_axis=1, concat_axis=0, tiled=True),
        lax.all_to_all(value, "narrow", split_axis=1, concat_axis=0, tiled=True),
    )
    groups = stretch_keys.shape[1] // HEAD_DIM
    per_group = queries.shape[1] // stretch_keys.shape[1]
    cached = cache_key.shape[0]
    span = tokens // wide_count
    start = wide_place * span
    own_keys = lax.dynamic_slice_in_dim(stretch_keys, start, span, 0)
    own_values = lax.dynamic_slice_in_dim(stretch_values, start, span, 0)
    keys_all = jnp.concatenate([to_groups(cache_key, groups), to_groups(own_keys, groups)], axis=1)
    values_all = jnp.concatenate(
        [to_groups(cache_value, groups), to_groups(own_values, groups)], axis=1
    )
    queries_grouped = heads_grouped(queries, groups, per_group)
    position = jnp.arange(tokens, dtype=jnp.int32)[:, None]
    cached_at = wide_place * cached + jnp.arange(cached, dtype=jnp.int32)[None, :]
    stretch_at = start + jnp.arange(span, dtype=jnp.int32)[None, :]
    usable = jnp.concatenate([cached_at >= visible_from[:, None], stretch_at <= position], axis=1)
    scores = (
        jnp.einsum("gptd,gkd->gptk", queries_grouped, keys_all, preferred_element_type=jnp.float32)
        * scale
    )
    scores = jnp.where(usable, scores, -1e30)
    local_top = jnp.max(scores, axis=-1)
    local_total = jnp.sum(jnp.where(usable, jnp.exp(scores - local_top[..., None]), 0.0), axis=-1)
    top, total = combined_all((local_top, local_total), "wide", merge_softmax)
    probs = jnp.where(usable, jnp.exp(scores - top[..., None]), 0.0) / total[..., None]
    probs_low = probs.astype(jnp.bfloat16)
    attended_part = jnp.einsum(
        "gptk,gkd->gptd", probs_low, values_all, preferred_element_type=jnp.float32
    )
    attended = wide_total(from_groups(attended_part)).astype(jnp.bfloat16)
    stream = residual.astype(jnp.float32)
    gain = norm_gain.astype(jnp.float32)
    squares = width_sum(jnp.sum(stream * stream, axis=1))
    rstd = lax.rsqrt(squares / D + EPSILON)[:, None]
    scaled = stream * rstd
    normed = (scaled * gain).astype(jnp.bfloat16)
    gate_part = jnp.dot(normed, w_gate, preferred_element_type=jnp.float32)
    up_part = jnp.dot(normed, w_up, preferred_element_type=jnp.float32)
    hidden_part = contract_cols(grad_out, w_down)
    gate, up, hidden_grad = width_sum((gate_part, up_part, hidden_part))
    activated, d_gate, d_up = swiglu_back(gate, up, hidden_grad)
    grad_w_down = contract_rows(activated, grad_out).astype(jnp.bfloat16)
    grad_w_gate = contract_rows(normed, d_gate).astype(jnp.bfloat16)
    grad_w_up = contract_rows(normed, d_up).astype(jnp.bfloat16)
    d_normed = wide_total(contract_cols(d_gate, w_gate) + contract_cols(d_up, w_up))
    grad_gain = jnp.sum(d_normed * scaled, axis=0)
    weighted = d_normed * gain
    inner = width_sum(jnp.sum(weighted * scaled, axis=1)) / D
    grad_residual = (
        grad_out.astype(jnp.float32) + rstd * (weighted - scaled * inner[:, None])
    ).astype(jnp.bfloat16)
    columns = w_output.shape[1]
    whole = lax.all_gather(grad_residual, "narrow", axis=1, tiled=True)
    panel = lax.dynamic_slice_in_dim(whole, wide_place * columns, columns, 1)
    d_attention = wide_total(contract_cols(panel, w_output)).astype(jnp.bfloat16)
    grad_w_output = contract_rows(attended, panel).astype(jnp.bfloat16)
    grads_grouped = heads_grouped(d_attention, groups, per_group)
    attended_grouped = heads_grouped(attended, groups, per_group)
    prob_grad = jnp.einsum(
        "gptd,gkd->gptk", grads_grouped, values_all, preferred_element_type=jnp.float32
    )
    delta = jnp.sum(
        grads_grouped.astype(jnp.float32) * attended_grouped.astype(jnp.float32), axis=-1
    )
    score_grad = (probs * (prob_grad - delta[..., None])).astype(jnp.bfloat16)
    query_part = (
        jnp.einsum("gptk,gkd->gptd", score_grad, keys_all, preferred_element_type=jnp.float32)
        * scale
    )
    grad_query = wide_total(from_groups(query_part)).astype(jnp.bfloat16)
    return (
        grad_residual,
        grad_gain,
        grad_w_gate,
        grad_w_up,
        grad_w_down,
        grad_w_output,
        grad_query,
    )


def solution(mesh):
    in_specs = (
        P(None, "narrow"),
        P("narrow"),
        P(None, "narrow"),
        P("narrow", "wide"),
        P("narrow", "wide"),
        P("wide", "narrow"),
        P("narrow", "wide"),
        P("narrow", None),
        P("narrow", None),
        P("narrow", None),
        P("wide", "narrow"),
        P("wide", "narrow"),
        P(),
    )
    out_specs = (
        P(None, "narrow"),
        P("narrow"),
        P("narrow", "wide"),
        P("narrow", "wide"),
        P("wide", "narrow"),
        P("narrow", "wide"),
        P(None, "narrow"),
    )
    return jax.shard_map(
        per_device, mesh=mesh, in_specs=in_specs, out_specs=out_specs, check_vma=False
    )
```

profile of v0, /device:TPU:0, one launch (start us, length us, event | category | flops | bytes accessed | tf_op | source)
XLA Modules:
  0.0 798.1 jit_solution(1576935629067620827)
XLA Ops:
  7.2 1.9 copy.110
  9.1 4.2 all-to-all-start
  14.0 2.1 fusion.17
  16.0 5.1 psum.63
  21.2 10.6 %fusion.45 = f32[384,1728]{0,1:T(8,128)} fusion(bf16[2560,1728]{0,1:T(8,128)(2,1)} %param.18, bf16[384,2560]{1,0:T(8,128)(2,1)} %param.15, f32[2560]{0:T(1024)S(1)} %convert_element_type.65, f32[384]{0:T(512)S(1)} %add_rsqrt_fusion), kind=kOutput, calls=%fused_computation.75 | convolution fusion | flops 3401318400 | bytes 13479424 | tf_op jit(solution)/shard_map/dot_general | solution.py:134
  31.9 6.4 fusion.47
  38.3 6.5 fusion.49
  44.9 4.4 copy.73
  49.3 4.0 copy.74
  53.3 3.1 copy.108
  57.1 3.9 copy.80
  61.0 4.0 copy.81
  65.1 3.5 all-to-all-start.2
  68.6 11.7 %all-to-all-done.2 = bf16[192,2,512]{2,0,1:T(8,128)(2,1)S(1)} async-done(((bf16[192,2,512]{2,0,1:T(8,128)(2,1)}), bf16[192,2,512]{2,0,1:T(8,128)(2,1)S(1)}, u32[]{:S(2)}, u32[]{:S(2)}) %all-to-all-start.2) | async-done | bytes 393248 | tf_op jit(solution)/shard_map/all_to_all | solution.py:96
  80.3 4.8 all-to-all-start.1
  86.1 44.3 %all-to-all-done.1 = bf16[192,2,2560]{2,0,1:T(8,128)(2,1)} async-done(((bf16[192,2,2560]{2,0,1:T(8,128)(2,1)}), bf16[192,2,2560]{2,0,1:T(8,128)(2,1)}, u32[]{:S(2)}, u32[]{:S(2)}) %all-to-all-start.1) | async-done | bytes 1966112 | tf_op jit(solution)/shard_map/all_to_all | solution.py:94
  130.4 5.7 reshape.86
  136.1 27.7 %fusion.2 = (f32[4,5,384]{2,1,0:T(8,128)S(1)}, f32[4,2072,5,384]{3,1,2,0:T(8,128)}) fusion(pred[384,2072]{0,1:T(8,128)(4,1)S(1)} %pad_add_fusion, bf16[384,4,5,128]{3,2,1,0:T(8,128)(2,1)} %reshape.86, bf16[4,24,128]{2,1,0:T(8,128)(2,1)S(1)} %bitcast_bitcast_fusion.1, bf16[4,2048,128]{2,1,0:T(8,128)(2,1)} %bitcast.131), kind=kOutput, calls=%fused_computation.9 | convolution fusion | flops 4125692416 | bytes 68566016 | tf_op jit(solution)/shard_map/gptd,gkd->gptk/dot_general | solution.py:115
  163.8 22.2 %select_reduce_fusion = f32[4,5,384]{2,1,0:T(8,128)S(1)} fusion(f32[4,2072,5,384]{3,1,2,0:T(8,128)} %get-tuple-element.164, f32[4,5,384]{2,1,0:T(8,128)S(1)} %get-tuple-element.163, pred[384,2072]{0,1:T(8,128)(4,1)S(1)} %pad_add_fusion), kind=kLoop, calls=%fused_computation.8 | loop fusion | flops 79557120 | bytes 64508928 | tf_op jit(solution)/shard_map/reduce_sum | solution.py:120
  186.0 24.1 %all-gather.1 = f32[64,5,384]{2,1,0:T(8,128)S(1)} all-gather(f32[4,5,384]{2,1,0:T(8,128)S(1)} %select_reduce_fusion), channel_id=3, replica_groups=mesh['wide'=16,'narrow'=2] {'wide'}, dimensions={0}, use_global_device_ids=true | all-gather | bytes 522240 | tf_op jit(solution)/shard_map/all_gather | solution.py:16
  211.0 19.6 %all-gather = f32[64,5,384]{2,1,0:T(8,128)S(1)} all-gather(f32[4,5,384]{2,1,0:T(8,128)S(1)} %get-tuple-element.163), channel_id=2, replica_groups=mesh['wide'=16,'narrow'=2] {'wide'}, dimensions={0}, use_global_device_ids=true | all-gather | bytes 522240 | tf_op jit(solution)/shard_map/all_gather | solution.py:16
  230.6 0.9 copy-done.11
  231.5 31.0 %all-reduce.9.cloned.1.call-done = (f32[384,1728]{0,1:T(8,128)}, f32[384,1728]{0,1:T(8,128)}, f32[384,1728]{0,1:T(8,128)}) async-done(((f32[384,1728]{0,1:T(8,128)}, f32[384,1728]{0,1:T(8,128)}, f32[384,1728]{0,1:T(8,128)}), (f32[384,1728]{0,1:T(8,128)}, f32[384,1728]{0,1:T(8,128)}, f32[384,1728]{0,1:T(8,128)})) %all-reduce.9.cloned.1.call-update) | async-done | bytes 7962640 | tf_op jit(solution)/shard_map/psum | solution.py:38
  262.5 4.7 multiply_convert_fusion.2
  267.2 7.1 fusion.50
  274.4 6.0 convolution_add_fusion
  280.5 13.5 %while.17 = (s32[]{:T(128)}, f32[4,5,384]{2,1,0:T(8,128)S(1)}, f32[4,5,384]{2,1,0:T(8,128)S(1)}, f32[16,4,5,384]{3,2,1,0:T(8,128)}, f32[16,4,5,384]{3,2,1,0:T(8,128)}, /*index=5*/s32[]{:T(128)}, s32[]{:T(128)}, s32[]{:T(128)}) while((s32[]{:T(128)}, f32[4,5,384]{2,1,0:T(8,128)S(1)}, f32[4,5,384]{2,1,0:T(8,128)S(1)}, ...), condition=%wide.region_12.13_spmd, body=%wide.region_11.12_spmd.sunk | while | flops 46085 | bytes 184451 | solution.py:22
  285.0 0.9 fusion.65
  285.9 0.9 fusion.65
  292.2 0.9 fusion.65
  293.9 95.7 %all-reduce.7.cloned.1.call-done = f32[384,2560]{1,0:T(8,128)} async-done(((f32[384,2560]{1,0:T(8,128)}), f32[384,2560]{1,0:T(8,128)}) %all-reduce.7.cloned.1.call-update) | async-done | bytes 3932176 | tf_op jit(solution)/shard_map/psum | solution.py:42
  389.7 4.5 fusion.16
  394.2 4.9 psum.68
  399.1 6.1 fusion.15
  405.2 31.3 %fusion.3 = f32[4,5,384,128]{2,3,1,0:T(8,128)} fusion(f32[4,2072,5,384]{3,1,2,0:T(8,128)} %get-tuple-element.164, f32[4,5,384]{2,1,0:T(8,128)S(1)} %get-tuple-element.141, f32[4,5,384]{2,1,0:T(8,128)S(1)} %get-tuple-element.140, pred[384,2072]{0,1:T(8,128)(4,1)} %copy-done.4, bf16[4,24,128]{2,1,0:T(8,128)(2,1)S(1)} %bitcast_bitcast_fusion, ...), kind=kOutput, calls=%fused_computation.10 | convolution fusion | flops 4173438976 | bytes 70562816 | tf_op jit(solution)/shard_map/gptk,gkd->gptd/dot_general | solution.py:124
  436.4 10.5 %convolution_convert_fusion = bf16[2560,1728]{0,1:T(8,128)(2,1)} fusion(bf16[384,1728]{0,1:T(8,128)(2,1)} %copy-done.3, bf16[384,2560]{1,0:T(8,128)(2,1)} %param.15, f32[2560]{0:T(1024)S(1)} %convert_element_type.65, f32[384]{0:T(512)S(1)} %add_rsqrt_fusion), kind=kOutput, calls=%fused_computation.13 | convolution fusion | flops 3405742080 | bytes 12152320 | tf_op jit(solution)/shard_map/dot_general | solution.py:26
  447.0 7.3 convolution_convert_fusion.1
  454.3 7.3 convolution_convert_fusion.2
  461.6 4.1 fusion.27
  465.7 169.5 %all-reduce.10 = (bf16[384,2560]{0,1:T(8,128)(2,1)}, bf16[384,2560]{1,0:T(8,128)(2,1)}) all-reduce(f32[384,2560]{0,1:T(8,128)} %bitcast.129, f32[384,2560]{1,0:T(8,128)} %fusion.27), channel_id=1, replica_groups=mesh['wide'=16,'narrow'=2] {'wide'}, use_global_device_ids=true, to_apply=%region_13.14 | all-reduce | flops 1966080 | bytes 11796480 | tf_op jit(solution)/shard_map/psum | solution.py:42
  635.2 4.0 copy.84
  639.2 4.0 copy.85
  643.2 4.3 copy.86
  647.4 3.9 fusion.18
  651.4 37.9 %fusion.20 = f32[4,5,384,128]{2,3,1,0:T(8,128)} fusion(f32[4,5,384]{2,1,0:T(8,128)S(1)} %fusion.18, f32[4,5,384]{2,1,0:T(8,128)S(1)} %get-tuple-element.141, f32[4,5,384]{2,1,0:T(8,128)S(1)} %get-tuple-element.140, f32[4,2072,5,384]{3,1,2,0:T(8,128)} %get-tuple-element.164, pred[384,2072]{0,1:T(8,128)(4,1)S(1)} %copy-done.5, ...), kind=kOutput, calls=%fused_computation.40 | convolution fusion | flops 8284209152 | bytes 74681344 | tf_op jit(solution)/shard_map/gptk,gkd->gptd/dot_general | solution.py:164
  689.3 5.4 copy.87
  694.7 92.6 %all-reduce.11 = bf16[384,2560]{1,0:T(8,128)(2,1)} all-reduce(f32[384,2560]{1,0:T(8,128)} %copy.87), channel_id=1, replica_groups=mesh['wide'=16,'narrow'=2] {'wide'}, use_global_device_ids=true, to_apply=%region_16.17 | all-reduce | flops 983040 | bytes 5898240 | tf_op jit(solution)/shard_map/psum | solution.py:42
  787.3 3.9 convolution_convert_fusion.3
  (85 shorter events, 14.1 us)
Async XLA Ops:
  7.2 454.4 %copy-start = (bf16[2560,320]{0,1:T(8,128)(2,1)S(1)}, bf16[2560,320]{0,1:T(8,128)(2,1)}, u32[]{:S(2)}) copy-start(bf16[2560,320]{0,1:T(8,128)(2,1)} %param.21) | copy-start | bytes 4915204
  9.1 56.0 %all-to-all-start = ((bf16[192,2,512]{2,0,1:T(8,128)(2,1)}), bf16[192,2,512]{2,0,1:T(8,128)(2,1)S(1)}, u32[]{:S(2)}, u32[]{:S(2)}) async-start(bf16[192,2,512]{2,0,1:T(8,128)(2,1)} %bitcast.117), calls=%async_computation | async-start | bytes 786432 | tf_op jit(solution)/shard_map/all_to_all | solution.py:95
  13.3 249.2 %all-reduce.9.cloned.1.call-start = ((), (), s32[]{:S(2)}) async-start(), calls=%async_computation.5 | async-start | bytes 15925248 | tf_op jit(solution)/shard_map/psum | solution.py:38
  14.0 17.9 %slice-start = ((s8[8847360]{0:T(1024)(128)(4,1)}), s8[458752]{0:T(1024)(128)(4,1)S(1)}, s32[]{:S(2)}) async-start(s8[8847360]{0:T(1024)(128)(4,1)} %bitcast.120), calls=%async_computation.6 | async-start | bytes 917504
  21.2 10.7 %copy-start.1 = (bf16[384,2560]{1,0:T(8,128)(2,1)S(1)}, bf16[384,2560]{1,0:T(8,128)(2,1)}, u32[]{:S(2)}) copy-start(bf16[384,2560]{1,0:T(8,128)(2,1)} %param.15) | copy-start | bytes 5898244
  21.2 10.7 %slice-start.1 = ((s8[8847360]{0:T(1024)(128)(4,1)}), s8[4194304]{0:T(1024)(128)(4,1)S(1)}, s32[]{:S(2)}) async-start(s8[8847360]{0:T(1024)(128)(4,1)} %bitcast.120), calls=%async_computation.7 | async-start | bytes 8388608
  21.2 10.7 %slice-start.2 = ((s8[8847360]{0:T(1024)(128)(4,1)}), s8[4194304]{0:T(1024)(128)(4,1)S(1)}, s32[]{:S(2)}) async-start(s8[8847360]{0:T(1024)(128)(4,1)} %bitcast.120), calls=%async_computation.8 | async-start | bytes 8388608
  21.2 17.1 %slice-start.6 = ((s8[8847360]{0:T(1024)(128)(4,1)}), s8[4194304]{0:T(1024)(128)(4,1)S(1)}, s32[]{:S(2)}) async-start(s8[8847360]{0:T(1024)(128)(4,1)} %bitcast.142), calls=%async_computation.12 | async-start | bytes 8388608
  21.2 17.1 %slice-start.7 = ((s8[8847360]{0:T(1024)(128)(4,1)}), s8[4194304]{0:T(1024)(128)(4,1)S(1)}, s32[]{:S(2)}) async-start(s8[8847360]{0:T(1024)(128)(4,1)} %bitcast.142), calls=%async_computation.13 | async-start | bytes 8388608
  31.9 6.4 copy-start.8
  31.9 6.4 slice-start.8
  49.3 7.1 copy-start.12
  61.0 24.2 %copy-start.15 = (s32[384]{0:T(512)S(1)}, s32[384]{0:T(512)}, u32[]{:S(2)}) copy-start(s32[384]{0:T(512)} %param.27) | copy-start | bytes 4612
  65.1 15.2 %all-to-all-start.2 = ((bf16[192,2,512]{2,0,1:T(8,128)(2,1)}), bf16[192,2,512]{2,0,1:T(8,128)(2,1)S(1)}, u32[]{:S(2)}, u32[]{:S(2)}) async-start(bf16[192,2,512]{2,0,1:T(8,128)(2,1)} %bitcast.116), calls=%async_computation.2 | async-start | bytes 786432 | tf_op jit(solution)/shard_map/all_to_all | solution.py:96
  80.3 50.1 %all-to-all-start.1 = ((bf16[192,2,2560]{2,0,1:T(8,128)(2,1)}), bf16[192,2,2560]{2,0,1:T(8,128)(2,1)}, u32[]{:S(2)}, u32[]{:S(2)}) async-start(bf16[192,2,2560]{2,0,1:T(8,128)(2,1)} %bitcast.126), calls=%async_computation.1 | async-start | bytes 3932160 | tf_op jit(solution)/shard_map/all_to_all | solution.py:94
  85.1 304.6 %all-reduce.7.cloned.1.call-start = ((), (), s32[]{:S(2)}) async-start(), calls=%async_computation.3 | async-start | bytes 7864320 | tf_op jit(solution)/shard_map/psum | solution.py:42
  86.1 77.7 %copy-start.4 = (pred[384,2072]{0,1:T(8,128)(4,1)}, pred[384,2072]{0,1:T(8,128)(4,1)S(1)}, u32[]{:S(2)}) copy-start(pred[384,2072]{0,1:T(8,128)(4,1)S(1)} %pad_add_fusion) | copy-start | bytes 2386948
  86.1 77.7 %copy-start.13 = (bf16[4,24,128]{2,1,0:T(8,128)(2,1)}, bf16[4,24,128]{2,1,0:T(8,128)(2,1)S(1)}, u32[]{:S(2)}) copy-start(bf16[4,24,128]{2,1,0:T(8,128)(2,1)S(1)} %bitcast_bitcast_fusion.1) | copy-start | bytes 73732
  210.2 0.9 copy-start.10
  230.6 0.9 copy-start.11
  262.5 11.8 %slice-start.3 = ((s8[8847360]{0:T(1024)(128)(4,1)}), s8[458752]{0:T(1024)(128)(4,1)S(1)}, s32[]{:S(2)}) async-start(s8[8847360]{0:T(1024)(128)(4,1)} %bitcast.122), calls=%async_computation.9 | async-start | bytes 917504
  262.5 11.8 %slice-start.4 = ((s8[8847360]{0:T(1024)(128)(4,1)}), s8[4194304]{0:T(1024)(128)(4,1)S(1)}, s32[]{:S(2)}) async-start(s8[8847360]{0:T(1024)(128)(4,1)} %bitcast.122), calls=%async_computation.10 | async-start | bytes 8388608
  267.2 7.1 copy-start.3
  267.2 7.1 slice-start.5
  280.4 181.2 %all-gather.4.cloned.1.call-start = ((), (), s32[]{:S(2)}) async-start(), calls=%async_computation.4 | async-start | bytes 5898240 | tf_op jit(solution)/shard_map/all_gather | solution.py:150
  436.4 10.5 %copy-start.2 = (bf16[384,2560]{1,0:T(8,128)(2,1)S(1)}, bf16[384,2560]{1,0:T(8,128)(2,1)}, u32[]{:S(2)}) copy-start(bf16[384,2560]{1,0:T(8,128)(2,1)} %param.15) | copy-start | bytes 5898244
  447.0 7.3 copy-start.6
  447.0 7.3 copy-start.7
  447.0 7.3 copy-start.9
  647.4 3.9 copy-start.5
  647.4 3.9 copy-start.14
Sparse Core Ops, SparseCore 0:
  45.0 217.4 all-reduce.8
  280.6 109.0 all-reduce.6
  405.3 52.3 all-gather.3
where the time goes:
time: 810 us; the launch traced here: 798 us
  blocking collectives  316 us (39%)
  waiting for transfers between devices  183 us (23%)
  matrix products  167 us (21%)
  other arithmetic  58.2 us (7%)
  local copies, waits for them, and re-layouts  47.3 us (6%)
  between operations  14.5 us (2%)
  starting transfers between devices  12.6 us (2%)
    psum x2, blocking collectives, wide_total(): return lax.psum(parts, 'wide')  262 us
    psum x1, waiting for transfers between devices, wide_total(): return lax.psum(parts, 'wide')  95.7 us
    all_to_all x1, waiting for transfers between devices, per_device(): lax.all_to_all(query, 'narrow', split_axis=1, concat_axis=0, tiled=True)  44.3 us
    all_gather x2, blocking collectives, combined_all(): everything = jax.tree.map(lambda part: lax.all_gather(part, axis), array)  43.7 us
    dot_general x1, matrix products, per_device(): jnp.einsum('gptk,gkd->gptd', score_grad, keys_all, preferred_element_type...  37.9 us
    dot_general x1, matrix products, per_device(): jnp.einsum('gptk,gkd->gptd', probs_low, values_all, preferred_element_typ...  31.3 us
    psum x1, waiting for transfers between devices, width_sum(): return lax.psum(parts, 'narrow')  31 us
    dot_general x4, matrix products, contract_rows(): lax.dot_general(left, right, (((0,), (0,)), ((), ())), preferred_element_...  29 us
  transfers between devices with their start and end apart: 6, of which 4 were waited for; matrix products, arithmetic and copies ran while one was open for 22% of the time, Pallas kernels for 0%

commit v1 on v0

v1 whole, which is shorter than its diff:
```python
import functools
import math

import jax
import jax.numpy as jnp
from jax import lax
from jax.experimental import pallas as pl
from jax.experimental.pallas import tpu as pltpu
from jax.sharding import PartitionSpec as P

D = 5120
HEAD_DIM = 128


EPSILON = 1e-06


def contract_rows(left, right):
    return lax.dot_general(
        left, right, (((0,), (0,)), ((), ())), preferred_element_type=jnp.float32
    )


def contract_cols(left, right):
    return lax.dot_general(
        left, right, (((1,), (1,)), ((), ())), preferred_element_type=jnp.float32
    )


def swapped(array, axis, bit):
    size = lax.axis_size(axis)
    return lax.ppermute(array, axis, [(i, i ^ (1 << bit)) for i in range(size)])


def wide_bits():
    return lax.axis_size("wide").bit_length() - 1


def bit_of(k):
    return (lax.axis_index("wide") >> k) & 1


def as_cube(array):
    count = lax.axis_size("wide")
    return array.reshape((2,) * wide_bits() + (array.shape[0] // count, array.shape[1]))


def scatter_sum(cube, order):
    for k in order:
        bit = bit_of(k)
        sent = lax.dynamic_slice_in_dim(cube, 1 - bit, 1, k).astype(jnp.bfloat16)
        kept = lax.dynamic_slice_in_dim(cube, bit, 1, k).astype(jnp.float32)
        cube = kept + swapped(sent, "wide", k).astype(jnp.float32)
    return cube.reshape(cube.shape[-2:])


def gathered(chunk, order):
    cube = chunk.reshape((1,) * wide_bits() + chunk.shape)
    for k in reversed(order):
        other = swapped(cube, "wide", k)
        first = bit_of(k) == 0
        cube = jnp.concatenate(
            [jnp.where(first, cube, other), jnp.where(first, other, cube)], axis=k
        )
    return cube.reshape(-1, cube.shape[-1])


def own_rows(array):
    bits = wide_bits()
    rows = array.shape[0] // lax.axis_size("wide")
    at = sum(bit_of(k) << (bits - 1 - k) for k in range(bits))
    return lax.dynamic_slice_in_dim(array, at * rows, rows, 0)


def doubled(value, combine):
    for k in range(wide_bits()):
        value = combine(value, swapped(value, "wide", k))
    return value


def orders():
    bits = wide_bits()
    plain = list(range(bits))
    return (plain, plain[:1] + plain[2:] + plain[1:2])


def narrow_sum(part):
    if lax.axis_size("narrow") == 2:
        return part + swapped(part, "narrow", 0)
    return lax.psum(part, "narrow")


def narrow_total(part):
    if lax.axis_size("narrow") == 2:
        return part + swapped(part.astype(jnp.bfloat16), "narrow", 0).astype(jnp.float32)
    return lax.psum(part, "narrow")


def to_heads(rows):
    if lax.axis_size("narrow") != 2:
        return lax.all_to_all(rows, "narrow", split_axis=1, concat_axis=0, tiled=True)
    place = lax.axis_index("narrow")
    half = rows.shape[1] // 2
    count = rows.shape[0] // 2
    bit = bit_of(0)
    kept = lax.dynamic_slice_in_dim(rows, place * half, half, 1)
    sent = lax.dynamic_slice(rows, (bit * count, (1 - place) * half), (count, half))
    got = swapped(sent, "narrow", 0)
    other = swapped(got, "wide", 0)
    first = bit == 0
    far = jnp.concatenate([jnp.where(first, got, other), jnp.where(first, other, got)], axis=0)
    low = place == 0
    return jnp.concatenate([jnp.where(low, kept, far), jnp.where(low, far, kept)], axis=0)


def merge_softmax(base, first, second):
    heads = first.shape[1] // 2
    top = jnp.maximum(first[:, :heads], second[:, :heads])
    total = first[:, heads:] * jnp.exp2((first[:, :heads] - top) * base) + second[
        :, heads:
    ] * jnp.exp2((second[:, :heads] - top) * base)
    return jnp.concatenate([top, total], axis=1)


def swiglu_back(gate, up, hidden_grad):
    sigmoid_gate = jax.nn.sigmoid(gate)
    silu_gate = gate * sigmoid_gate
    activated = (silu_gate * up).astype(jnp.bfloat16)
    d_gate = (hidden_grad * up * sigmoid_gate * (1.0 + gate * (1.0 - sigmoid_gate))).astype(
        jnp.bfloat16
    )
    d_up = (hidden_grad * silu_gate).astype(jnp.bfloat16)
    return (activated, d_gate, d_up)


LOG2E = 1.4426950408889634
MASKED = -1e30


def raw_scores(q, key_ref, own_key_ref, from_ref, own_ref):
    cached = contract_cols(q, key_ref[...])
    at = lax.broadcasted_iota(jnp.int32, cached.shape, 1)
    cached = jnp.where(at >= from_ref[...], cached, MASKED)
    own = contract_cols(q, own_key_ref[...])
    own_at = lax.broadcasted_iota(jnp.int32, own.shape, 1)
    own = jnp.where(own_at <= own_ref[...], own, MASKED)
    return (cached, own)


def pick_lane(stat_ref, head):
    lane = lax.broadcasted_iota(jnp.int32, stat_ref.shape, 1)
    return jnp.sum(jnp.where(lane == head, stat_ref[...], 0.0), axis=1, keepdims=True)


def forward_kernel(
    base, q_ref, key_ref, value_ref, own_key_ref, own_value_ref,
    from_ref, own_ref, out_ref, top_ref, total_ref,
):
    head = pl.program_id(0)

    @pl.when(head == 0)
    def _():
        top_ref[...] = jnp.zeros_like(top_ref)
        total_ref[...] = jnp.zeros_like(total_ref)

    cached, own = raw_scores(q_ref[...], key_ref, own_key_ref, from_ref, own_ref)
    top = jnp.maximum(
        jnp.max(cached, axis=1, keepdims=True), jnp.max(own, axis=1, keepdims=True)
    )
    cached = jnp.exp2((cached - top) * base)
    own = jnp.exp2((own - top) * base)
    total = jnp.sum(cached, axis=1, keepdims=True) + jnp.sum(own, axis=1, keepdims=True)
    out = jnp.dot(
        cached.astype(jnp.bfloat16), value_ref[...], preferred_element_type=jnp.float32
    ) + jnp.dot(
        own.astype(jnp.bfloat16), own_value_ref[...], preferred_element_type=jnp.float32
    )
    out_ref[...] = out.astype(out_ref.dtype)
    lane = lax.broadcasted_iota(jnp.int32, top_ref.shape, 1)
    top_ref[...] = jnp.where(lane == head, top, top_ref[...])
    total_ref[...] = jnp.where(lane == head, total, total_ref[...])


def backward_kernel(
    first_head, base, scale, q_ref, grad_ref, attended_ref, key_ref, value_ref,
    own_key_ref, own_value_ref, from_ref, own_ref, top_ref, inverse_ref, out_ref,
):
    head = first_head + pl.program_id(0)
    cached, own = raw_scores(q_ref[...], key_ref, own_key_ref, from_ref, own_ref)
    top = pick_lane(top_ref, head)
    inverse = pick_lane(inverse_ref, head)
    grad = grad_ref[...]
    delta = jnp.sum(
        grad.astype(jnp.float32) * attended_ref[...].astype(jnp.float32),
        axis=1,
        keepdims=True,
    )
    cached = jnp.exp2((cached - top) * base) * (contract_cols(grad, value_ref[...]) - delta)
    own = jnp.exp2((own - top) * base) * (contract_cols(grad, own_value_ref[...]) - delta)
    out = jnp.dot(
        cached.astype(jnp.bfloat16), key_ref[...], preferred_element_type=jnp.float32
    ) + jnp.dot(
        own.astype(jnp.bfloat16), own_key_ref[...], preferred_element_type=jnp.float32
    )
    out_ref[...] = (out * (inverse * scale)).astype(out_ref.dtype)


def blocks(tokens, cached, padded, group, first):
    head = pl.BlockSpec((tokens, HEAD_DIM), lambda p: (0, first + p))
    rows = pl.BlockSpec((cached, HEAD_DIM), lambda p: (0, group))
    own = pl.BlockSpec((padded, HEAD_DIM), lambda p: (0, group))
    bound = pl.BlockSpec((tokens, 1), lambda p: (0, 0))
    stat = pl.BlockSpec((tokens, HEAD_DIM), lambda p: (0, 0))
    return (head, rows, own, bound, stat)


def forward_group(group, per_group, base, queries, keys, values, own_keys, own_values, bounds):
    tokens = queries.shape[0]
    cached, padded = keys.shape[0], own_keys.shape[0]
    head, rows, own, bound, stat = blocks(tokens, cached, padded, group, group * per_group)
    out = pl.BlockSpec((tokens, HEAD_DIM), lambda p: (0, p))
    work = per_group * tokens * (cached + padded)
    return pl.pallas_call(
        functools.partial(forward_kernel, base),
        grid=(per_group,),
        in_specs=[head, rows, rows, own, own, bound, bound],
        out_specs=[out, stat, stat],
        out_shape=[
            jax.ShapeDtypeStruct((tokens, per_group * HEAD_DIM), jnp.float32),
            jax.ShapeDtypeStruct((tokens, HEAD_DIM), jnp.float32),
            jax.ShapeDtypeStruct((tokens, HEAD_DIM), jnp.float32),
        ],
        compiler_params=pltpu.CompilerParams(vmem_limit_bytes=40 << 20),
        cost_estimate=pl.CostEstimate(
            flops=4 * HEAD_DIM * work, bytes_accessed=6 << 20, transcendentals=work
        ),
    )(queries, keys, values, own_keys, own_values, *bounds)


def backward_group(
    group, per_group, base, scale, queries, grads, attended, keys, values,
    own_keys, own_values, bounds, top, inverse, shift,
):
    tokens = queries.shape[0]
    cached, padded = keys.shape[0], own_keys.shape[0]
    first = group * per_group
    head, rows, own, bound, stat = blocks(tokens, cached, padded, group, first)
    grad = pl.BlockSpec((tokens, HEAD_DIM), lambda p: (0, first - shift + p))
    out = pl.BlockSpec((tokens, HEAD_DIM), lambda p: (0, p))
    work = per_group * tokens * (cached + padded)
    return pl.pallas_call(
        functools.partial(backward_kernel, first, base, scale),
        grid=(per_group,),
        in_specs=[head, grad, head, rows, rows, own, own, bound, bound, stat, stat],
        out_specs=out,
        out_shape=jax.ShapeDtypeStruct((tokens, per_group * HEAD_DIM), jnp.float32),
        compiler_params=pltpu.CompilerParams(vmem_limit_bytes=48 << 20),
        cost_estimate=pl.CostEstimate(
            flops=6 * HEAD_DIM * work, bytes_accessed=6 << 20, transcendentals=work
        ),
    )(queries, grads, attended, keys, values, own_keys, own_values, *bounds, top, inverse)


def split_columns(array, pieces):
    width = array.shape[1] // pieces
    return [array[:, i * width : (i + 1) * width] for i in range(pieces)]


def per_device(
    residual,
    norm_gain,
    grad_out,
    w_gate,
    w_up,
    w_down,
    w_output,
    query,
    key,
    value,
    cache_key,
    cache_value,
    visible_from,
):
    wide_count = lax.axis_size("wide")
    wide_place = lax.axis_index("wide")
    tokens = residual.shape[0]
    scale = 1.0 / math.sqrt(HEAD_DIM)
    base = scale * LOG2E

    stream = residual.astype(jnp.float32)
    gain = norm_gain.astype(jnp.float32)
    hidden_part = contract_cols(grad_out, w_down)
    squares = narrow_sum(jnp.sum(stream * stream, axis=1))
    rstd = lax.rsqrt(squares / D + EPSILON)[:, None]
    normed = (stream * rstd * gain).astype(jnp.bfloat16)
    gate_part = jnp.dot(normed, w_gate, preferred_element_type=jnp.float32)
    up_part = jnp.dot(normed, w_up, preferred_element_type=jnp.float32)

    queries, stretch_keys, stretch_values = (to_heads(query), to_heads(key), to_heads(value))
    groups = stretch_keys.shape[1] // HEAD_DIM
    per_group = queries.shape[1] // stretch_keys.shape[1]
    heads = groups * per_group
    cached = cache_key.shape[0]
    span = tokens // wide_count
    start = wide_place * span
    padded = -(-span // HEAD_DIM) * HEAD_DIM
    filler = ((0, padded - span), (0, 0))
    own_keys = jnp.pad(lax.dynamic_slice_in_dim(stretch_keys, start, span, 0), filler)
    own_values = jnp.pad(lax.dynamic_slice_in_dim(stretch_values, start, span, 0), filler)
    position = jnp.arange(tokens, dtype=jnp.int32)[:, None]
    bounds = (
        visible_from[:, None] - wide_place * cached,
        jnp.minimum(position - start, span - 1),
    )

    hidden_grad = narrow_total(hidden_part)
    gate = narrow_total(gate_part)
    up = narrow_total(up_part)

    outs, tops, totals = [], [], []
    for group in range(groups):
        out, top, total = forward_group(
            group, per_group, base, queries, cache_key, cache_value, own_keys, own_values, bounds
        )
        outs.append(out)
        tops.append(top[:, :per_group])
        totals.append(total[:, :per_group])
    local_top = jnp.concatenate(tops, axis=1)
    stats = doubled(
        jnp.concatenate([local_top] + totals, axis=1), functools.partial(merge_softmax, base)
    )
    top, inverse = stats[:, :heads], 1.0 / stats[:, heads:]
    factor = jnp.exp2((local_top - top) * base) * inverse
    spread = jnp.repeat(factor, HEAD_DIM, axis=1)
    attended_part = jnp.concatenate(outs, axis=1) * spread
    side = ((0, 0), (0, HEAD_DIM - heads))
    top, inverse = jnp.pad(top, side), jnp.pad(inverse, side)
    ways = orders()
    attended = jnp.concatenate(
        [
            gathered(scatter_sum(as_cube(part), way).astype(jnp.bfloat16), way)
            for part, way in zip(split_columns(attended_part, 2), ways)
        ],
        axis=1,
    )

    activated, d_gate, d_up = swiglu_back(gate, up, hidden_grad)
    d_normed_part = contract_cols(d_gate, w_gate) + contract_cols(d_up, w_up)
    grad_w_down = contract_rows(activated, grad_out).astype(jnp.bfloat16)
    grad_w_gate = contract_rows(normed, d_gate).astype(jnp.bfloat16)
    grad_w_up = contract_rows(normed, d_up).astype(jnp.bfloat16)
    d_normed = jnp.concatenate(
        [
            scatter_sum(as_cube(part), way)
            for part, way in zip(split_columns(d_normed_part, 2), ways)
        ],
        axis=1,
    )
    rstd_rows = own_rows(rstd)
    scaled = own_rows(residual).astype(jnp.float32) * rstd_rows
    grad_gain = doubled(jnp.sum(d_normed * scaled, axis=0), jnp.add)
    weighted = d_normed * gain
    inner = narrow_sum(jnp.sum(weighted * scaled, axis=1)) / D
    grad_rows = (
        own_rows(grad_out).astype(jnp.float32)
        + rstd_rows * (weighted - scaled * inner[:, None])
    ).astype(jnp.bfloat16)
    grad_residual = jnp.concatenate(
        [gathered(part, way) for part, way in zip(split_columns(grad_rows, 2), ways)], axis=1
    )

    columns = w_output.shape[1]
    width = grad_residual.shape[1]
    if lax.axis_size("narrow") == 2:
        own_panel = lax.dynamic_slice_in_dim(
            grad_residual, (wide_place * columns) % width, columns, 1
        )
        holder = (wide_place * columns) // width == lax.axis_index("narrow")
        panel = jnp.where(holder, own_panel, swapped(own_panel, "narrow", 0))
    else:
        whole = lax.all_gather(grad_residual, "narrow", axis=1, tiled=True)
        panel = lax.dynamic_slice_in_dim(whole, wide_place * columns, columns, 1)
    grad_w_output = contract_rows(attended, panel).astype(jnp.bfloat16)

    pieces = 2 if groups % 2 == 0 else 1
    group_count = groups // pieces
    query_grads = []
    for piece in range(pieces):
        way = ways[piece]
        wide_rows = group_count * per_group * HEAD_DIM
        rows = w_output[piece * wide_rows : (piece + 1) * wide_rows]
        d_attention = gathered(
            scatter_sum(as_cube(contract_cols(panel, rows)), way).astype(jnp.bfloat16), way
        )
        parts = [
            backward_group(
                group, per_group, base, scale, queries, d_attention, attended, cache_key,
                cache_value, own_keys, own_values, bounds, top, inverse,
                piece * group_count * per_group,
            )
            for group in range(piece * group_count, (piece + 1) * group_count)
        ]
        query_part = jnp.concatenate(parts, axis=1)
        query_grads.append(
            gathered(scatter_sum(as_cube(query_part), way).astype(jnp.bfloat16), way)
        )
    grad_query = jnp.concatenate(query_grads, axis=1)
    return (
        grad_residual,
        grad_gain,
        grad_w_gate,
        grad_w_up,
        grad_w_down,
        grad_w_output,
        grad_query,
    )


def solution(mesh):
    in_specs = (
        P(None, "narrow"),
        P("narrow"),
        P(None, "narrow"),
        P("narrow", "wide"),
        P("narrow", "wide"),
        P("wide", "narrow"),
        P("narrow", "wide"),
        P("narrow", None),
        P("narrow", None),
        P("narrow", None),
        P("wide", "narrow"),
        P("wide", "narrow"),
        P(),
    )
    out_specs = (
        P(None, "narrow"),
        P("narrow"),
        P("narrow", "wide"),
        P("narrow", "wide"),
        P("wide", "narrow"),
        P("narrow", "wide"),
        P(None, "narrow"),
    )
    return jax.shard_map(
        per_device, mesh=mesh, in_specs=in_specs, out_specs=out_specs, check_vma=False
    )
```

time: 810 us -> 481 us (0.59)
  blocking collectives: 316 us -> 0 us
  Pallas kernels: 0 us -> 102 us
  matrix products: 167 us -> 69.3 us
  starting transfers between devices: 12.6 us -> 78.9 us
  other arithmetic: 58.2 us -> 32.1 us
  waiting for transfers between devices: 183 us -> 159 us
  local copies, waits for them, and re-layouts: 47.3 us -> 27.1 us
  between operations: 14.5 us -> 2.74 us
    psum x4 -> x0, blocking collectives: 272 us -> none  [the longest x2 262 us: wide_total(): return lax.psum(parts, 'wide')]
    ppermute x0 -> x84, waiting for transfers between devices: none -> 159 us  [swapped(): return lax.ppermute(array, axis, [(i, i ^ 1 << bit) for i in range(size)])]
    psum x2 -> x0, waiting for transfers between devices: 127 us -> none  [the longest x1 95.7 us: wide_total(): return lax.psum(parts, 'wide')]
    pallas_call x0 -> x8, Pallas kernels: none -> 102 us  [the longest x4 51.4 us: backward_group(): pl.pallas_call(functools.partial(backward_kernel, first, base, scale), gr...]
    dot_general x3 -> x0, matrix products: 96.8 us -> none  [the longest x1 37.9 us: per_device(): jnp.einsum('gptk,gkd->gptd', score_grad, keys_all, preferred_element_type...]
    ppermute x0 -> x84, starting transfers between devices: none -> 78.9 us  [swapped(): return lax.ppermute(array, axis, [(i, i ^ 1 << bit) for i in range(size)])]
    all_to_all x3 -> x0, waiting for transfers between devices: 56 us -> none  [the longest x1 44.3 us: per_device(): lax.all_to_all(query, 'narrow', split_axis=1, concat_axis=0, tiled=True)]
    all_gather x2 -> x0, blocking collectives: 43.7 us -> none  [combined_all(): everything = jax.tree.map(lambda part: lax.all_gather(part, axis), array)]
  transfers between devices with their start and end apart: 6 -> 84, of which waited for: 4 -> 49; matrix products, arithmetic and copies ran while one was open for 22% -> 24% of each run, Pallas kernels for 0% -> 16%
where the time goes in v1:
time: 481 us; the launch traced here: 472 us
  waiting for transfers between devices  159 us (33%)
  Pallas kernels  102 us (21%)
  starting transfers between devices  78.9 us (16%)
  matrix products  69.3 us (14%)
  other arithmetic  32.1 us (7%)
  local copies, waits for them, and re-layouts  27.1 us (6%)
    ppermute x84, waiting for transfers between devices, swapped(): return lax.ppermute(array, axis, [(i, i ^ 1 << bit) for i in range(size)])  159 us
    ppermute x84, starting transfers between devices, swapped(): return lax.ppermute(array, axis, [(i, i ^ 1 << bit) for i in range(size)])  78.9 us
    pallas_call x4, Pallas kernels, backward_group(): pl.pallas_call(functools.partial(backward_kernel, first, base, scale), gr...  51.4 us
    pallas_call x4, Pallas kernels, forward_group(): pl.pallas_call(functools.partial(forward_kernel, base), grid=(per_group,)...  51 us
    dot_general x4, matrix products, contract_rows(): lax.dot_general(left, right, (((0,), (0,)), ((), ())), preferred_element_...  30.2 us
    dot_general x5, matrix products, contract_cols(): lax.dot_general(left, right, (((1,), (1,)), ((), ())), preferred_element_...  22.7 us
    dot_general x1, matrix products, per_device(): gate_part = jnp.dot(normed, w_gate, preferred_element_type=jnp.float32)  10 us
  transfers between devices with their start and end apart: 84, of which 49 were waited for; matrix products, arithmetic and copies ran while one was open for 24% of the time, Pallas kernels for 16%

profile of v1, /device:TPU:0, one launch (start us, length us, event | category | flops | bytes accessed | tf_op | source)
XLA Modules:
  0.0 471.7 jit_solution(5467131824685054608)
XLA Ops:
  2.8 3.0 collective-permute-start
  14.6 9.0 %collective-permute-done.25 = bf16[96,2560]{1,0:T(8,128)(2,1)S(1)} collective-permute-done((bf16[96,2560]{1,0:T(8,128)(2,1)S(1)}, bf16[96,2560]{1,0:T(8,128)(2,1)S(1)}, u32[]{:S(2)}, u32[]{:S(2)}) %collective-permute-start.25) | collective-permute-done | bytes 491552 | tf_op jit(solution)/shard_map/ppermute | solution.py:32
  27.8 12.7 %shard_map.183 = (f32[384,640]{1,0:T(8,128)S(1)}, f32[384,128]{1,0:T(8,128)S(1)}, f32[384,128]{1,0:T(8,128)S(1)}) custom-call(bf16[384,2560]{1,0:T(8,128)(2,1)S(1)} %pad_maximum_fusion.1.q_ref, bf16[2048,512]{1,0:T(8,128)(2,1)S(1)} %copy-done.17, bf16[2048,512]{1,0:T(8,128)(2,1)S(1)} %copy-done.18, bf16[128,512]{1,0:T(8,128)(2,1)S(1)} %pad.14.own_key_ref, ...), custom_call_target="tpu_custom_call" | custom-call | flops 2139095040 | bytes 6291456 | tf_op jit(solution)/shard_map/pallas_call | solution.py:223
  41.5 12.7 %shard_map.182 = (f32[384,640]{1,0:T(8,128)S(1)}, f32[384,128]{1,0:T(8,128)S(1)}, f32[384,128]{1,0:T(8,128)S(1)}) custom-call(bf16[384,2560]{1,0:T(8,128)(2,1)S(1)} %pad_maximum_fusion.1.q_ref, bf16[2048,512]{1,0:T(8,128)(2,1)S(1)} %copy-done.17, bf16[2048,512]{1,0:T(8,128)(2,1)S(1)} %copy-done.18, bf16[128,512]{1,0:T(8,128)(2,1)S(1)} %pad.14.own_key_ref, ...), custom_call_target="tpu_custom_call" | custom-call | flops 2139095040 | bytes 6291456 | tf_op jit(solution)/shard_map/pallas_call | solution.py:223
  55.8 12.7 %shard_map.181 = (f32[384,640]{1,0:T(8,128)S(1)}, f32[384,128]{1,0:T(8,128)S(1)}, f32[384,128]{1,0:T(8,128)S(1)}) custom-call(bf16[384,2560]{1,0:T(8,128)(2,1)S(1)} %pad_maximum_fusion.1.q_ref, bf16[2048,512]{1,0:T(8,128)(2,1)S(1)} %copy-done.17, bf16[2048,512]{1,0:T(8,128)(2,1)S(1)} %copy-done.18, bf16[128,512]{1,0:T(8,128)(2,1)S(1)} %pad.14.own_key_ref, ...), custom_call_target="tpu_custom_call" | custom-call | flops 2139095040 | bytes 6291456 | tf_op jit(solution)/shard_map/pallas_call | solution.py:223
  71.0 12.9 %shard_map.180 = (f32[384,640]{1,0:T(8,128)S(1)}, f32[384,128]{1,0:T(8,128)S(1)}, f32[384,128]{1,0:T(8,128)S(1)}) custom-call(bf16[384,2560]{1,0:T(8,128)(2,1)S(1)} %pad_maximum_fusion.1.q_ref, bf16[2048,512]{1,0:T(8,128)(2,1)S(1)} %copy-done.17, bf16[2048,512]{1,0:T(8,128)(2,1)S(1)} %copy-done.18, bf16[128,512]{1,0:T(8,128)(2,1)S(1)} %pad.14.own_key_ref, ...), custom_call_target="tpu_custom_call" | custom-call | flops 2139095040 | bytes 6291456 | tf_op jit(solution)/shard_map/pallas_call | solution.py:223
  88.7 10.8 %fusion.26 = (bf16[384,1728]{0,1:T(8,128)(2,1)}, f32[384,1728]{0,1:T(8,128)}) fusion(bf16[384,2560]{1,0:T(8,128)(2,1)} %param.15, bf16[1728,2560]{1,0:T(8,128)(2,1)} %param.18), kind=kOutput, calls=%fused_computation.248 | convolution fusion | flops 3398049792 | bytes 14794752 | tf_op jit(solution)/shard_map/dot_general | solution.py:25
  105.5 4.5 collective-permute-done.32
  112.2 10.0 %fusion.27 = (bf16[384,1728]{0,1:T(8,128)(2,1)}, f32[384,1728]{0,1:T(8,128)}) fusion(bf16[2560,1728]{0,1:T(8,128)(2,1)} %param.16, bf16[384,2560]{1,0:T(8,128)(2,1)S(1)} %copy-done.21, f32[2560]{0:T(1024)S(1)} %convert_element_type.283, f32[384]{0:T(512)S(1)} %add_rsqrt_fusion), kind=kOutput, calls=%fused_computation.249 | convolution fusion | flops 3401981952 | bytes 14806528 | tf_op jit(solution)/shard_map/dot_general | solution.py:296
  124.4 2.7 collective-permute-start.34
  127.2 6.4 %fusion.28 = (bf16[384,1728]{0,1:T(8,128)(2,1)}, f32[384,1728]{0,1:T(8,128)}) fusion(bf16[2560,1728]{0,1:T(8,128)(2,1)S(1)} %bitcast.79, bf16[384,2560]{1,0:T(8,128)(2,1)S(1)} %copy-done.21, f32[2560]{0:T(1024)S(1)} %convert_element_type.283, f32[384]{0:T(512)S(1)} %add_rsqrt_fusion), kind=kOutput, calls=%fused_computation.250 | convolution fusion | flops 3401981952 | bytes 14806528 | tf_op jit(solution)/shard_map/dot_general | solution.py:297
  135.4 2.9 broadcast_in_dim.2
  138.4 5.8 %copy.85 = f32[384,2560]{1,0:T(8,128)} copy(f32[384,2560]{0,1:T(8,128)} %bitcast.75) | data formatting | bytes 7864320 | tf_op jit(solution)/shard_map/reshape | solution.py:334
  144.2 3.5 maximum_multiply_fusion
  149.5 10.8 %collective-permute-done.3 = bf16[384,1728]{0,1:T(8,128)(2,1)} collective-permute-done((bf16[384,1728]{0,1:T(8,128)(2,1)}, bf16[384,1728]{0,1:T(8,128)(2,1)}, u32[]{:S(2)}, u32[]{:S(2)}) %collective-permute-start.3) | collective-permute-done | bytes 1327136 | tf_op jit(solution)/shard_map/ppermute | solution.py:32
  160.3 27.9 %collective-permute-done.2 = bf16[384,1728]{0,1:T(8,128)(2,1)} collective-permute-done((bf16[384,1728]{0,1:T(8,128)(2,1)}, bf16[384,1728]{0,1:T(8,128)(2,1)}, u32[]{:S(2)}, u32[]{:S(2)}) %collective-permute-start.2) | collective-permute-done | bytes 1327136 | tf_op jit(solution)/shard_map/ppermute | solution.py:32
  188.2 5.5 %multiply_convert_fusion.1 = (bf16[384,1728]{0,1:T(8,128)(2,1)S(1)}, bf16[384,1728]{0,1:T(8,128)(2,1)S(1)}) fusion(f32[384,1728]{0,1:T(8,128)S(1)} %copy-done.19, bf16[384,1728]{0,1:T(8,128)(2,1)} %collective-permute-done.1, f32[384,1728]{0,1:T(8,128)} %get-tuple-element.132, bf16[384,1728]{0,1:T(8,128)(2,1)} %collective-permute-done.3, ...), kind=kLoop, calls=%fused_computation.12 | loop fusion | flops 12607488 | bytes 14598144 | tf_op jit(solution)/shard_map/convert_element_type | solution.py:132
  193.7 4.0 fusion.29
  197.7 8.8 %convolution_convert_fusion = bf16[2560,1728]{0,1:T(8,128)(2,1)} fusion(bf16[384,1728]{0,1:T(8,128)(2,1)S(1)} %get-tuple-element.43, bf16[384,2560]{1,0:T(8,128)(2,1)} %param.13, f32[2560]{0:T(1024)S(1)} %convert_element_type.283, f32[384]{0:T(512)S(1)} %copy-done.28), kind=kOutput, calls=%fused_computation | convolution fusion | flops 3405742080 | bytes 12152320 | tf_op jit(solution)/shard_map/dot_general | solution.py:19
  206.6 6.5 %convolution_add_fusion = f32[384,2560]{1,0:T(8,128)S(1)} fusion(f32[384,2560]{1,0:T(8,128)S(1)} %fusion.29, bf16[384,1728]{0,1:T(8,128)(2,1)S(1)} %get-tuple-element.43, bf16[2560,1728]{0,1:T(8,128)(2,1)} %param.17), kind=kOutput, calls=%fused_computation.5 | convolution fusion | flops 3398369280 | bytes 18038784 | tf_op jit(solution)/shard_map/dot_general | solution.py:25
  215.0 11.6 %convolution_convert_fusion.2 = bf16[1728,2560]{1,0:T(8,128)(2,1)} fusion(bf16[384,2560]{1,0:T(8,128)(2,1)} %param.15, f32[384,1728]{0,1:T(8,128)} %get-tuple-element.134, bf16[384,1728]{0,1:T(8,128)(2,1)} %collective-permute-done.2, f32[384,1728]{0,1:T(8,128)S(1)} %copy-done.20, bf16[384,1728]{0,1:T(8,128)(2,1)} %collective-permute-done.3), kind=kOutput, calls=%fused_computation.2 | convolution fusion | flops 3408445440 | bytes 18776064 | tf_op jit(solution)/shard_map/dot_general | solution.py:19
  226.7 7.5 %convolution_convert_fusion.1 = bf16[2560,1728]{0,1:T(8,128)(2,1)} fusion(bf16[384,1728]{0,1:T(8,128)(2,1)S(1)} %get-tuple-element.44, bf16[384,2560]{1,0:T(8,128)(2,1)S(1)} %copy-done.22, f32[2560]{0:T(1024)S(1)} %copy-done.26, f32[384]{0:T(512)S(1)} %copy-done.28), kind=kOutput, calls=%fused_computation.1 | convolution fusion | flops 3405742080 | bytes 12152320 | tf_op jit(solution)/shard_map/dot_general | solution.py:19
  243.5 2.6 collective-permute-start.37
  246.9 2.7 collective-permute-start.45
  251.6 3.1 collective-permute-done.9
  254.8 2.7 collective-permute-start.10
  261.2 5.0 %collective-permute-done.38 = bf16[1,1,1,1,24,1280]{5,4,3,2,1,0:T(8,128)(2,1)S(1)} collective-permute-done((bf16[1,1,1,1,24,1280]{5,4,3,2,1,0:T(8,128)(2,1)S(1)}, bf16[1,1,1,1,24,1280]{5,4,3,2,1,0:T(8,128)(2,1)S(1)}, u32[]{:S(2)}, u32[]{:S(2)}) %collective-permute-start.38) | collective-permute-done | bytes 61472 | tf_op jit(solution)/shard_map/ppermute | solution.py:32
  267.5 3.0 collective-permute-start.7
  276.0 2.7 collective-permute-done.12
  291.0 2.9 collective-permute-done.24
  295.3 3.6 collective-permute-start.41
  308.1 2.9 collective-permute-done.19
  317.4 6.2 %collective-permute-done.51 = bf16[384,320]{1,0:T(8,128)(2,1)S(1)} collective-permute-done((bf16[384,320]{1,0:T(8,128)(2,1)S(1)}, bf16[384,320]{1,0:T(8,128)(2,1)S(1)}, u32[]{:S(2)}, u32[]{:S(2)}) %collective-permute-start.51) | collective-permute-done | bytes 245792 | tf_op jit(solution)/shard_map/ppermute | solution.py:32
  329.4 6.6 %collective-permute-done.69 = bf16[1,2,1,2,24,1280]{5,4,3,2,1,0:T(8,128)(2,1)S(1)} collective-permute-done((bf16[1,2,1,2,24,1280]{5,4,3,2,1,0:T(8,128)(2,1)S(1)}, bf16[1,2,1,2,24,1280]{5,4,3,2,1,0:T(8,128)(2,1)S(1)}, u32[]{:S(2)}, u32[]{:S(2)}) %collective-permute-start.69) | collective-permute-done | bytes 245792 | tf_op jit(solution)/shard_map/ppermute | solution.py:32
  338.1 6.0 %collective-permute-done.70 = bf16[1,2,1,1,24,1280]{5,4,3,2,1,0:T(8,128)(2,1)S(1)} collective-permute-done((bf16[1,2,1,1,24,1280]{5,4,3,2,1,0:T(8,128)(2,1)S(1)}, bf16[1,2,1,1,24,1280]{5,4,3,2,1,0:T(8,128)(2,1)S(1)}, u32[]{:S(2)}, u32[]{:S(2)}) %collective-permute-start.70) | collective-permute-done | bytes 122912 | tf_op jit(solution)/shard_map/ppermute | solution.py:32
  345.4 3.0 collective-permute-done.71
  353.7 3.9 collective-permute-done.56
  357.7 2.9 collective-permute-done.73
  364.4 3.6 collective-permute-done.74
  370.2 13.1 %shard_map.187 = f32[384,640]{1,0:T(8,128)S(1)} custom-call(bf16[384,2560]{1,0:T(8,128)(2,1)S(1)} %pad_maximum_fusion.1.q_ref, bf16[384,1280]{1,0:T(8,128)(2,1)S(1)} %bitcast.57, bf16[384,2560]{1,0:T(8,128)(2,1)} %pad_maximum_fusion.2.attended_ref, bf16[2048,512]{1,0:T(8,128)(2,1)} %key_ref.15, bf16[2048,512]{1,0:T(8,128)(2,1)} %value_ref.15, ...), custom_call_target="tpu_custom_call" | custom-call | flops 3208642560 | bytes 6291456 | tf_op jit(solution)/shard_map/pallas_call | solution.py:251
  383.3 12.8 %shard_map.186 = f32[384,640]{1,0:T(8,128)S(1)} custom-call(bf16[384,2560]{1,0:T(8,128)(2,1)S(1)} %pad_maximum_fusion.1.q_ref, bf16[384,1280]{1,0:T(8,128)(2,1)S(1)} %bitcast.58, bf16[384,2560]{1,0:T(8,128)(2,1)} %pad_maximum_fusion.2.attended_ref, bf16[2048,512]{1,0:T(8,128)(2,1)} %key_ref.15, bf16[2048,512]{1,0:T(8,128)(2,1)} %value_ref.15, ...), custom_call_target="tpu_custom_call" | custom-call | flops 3208642560 | bytes 6291456 | tf_op jit(solution)/shard_map/pallas_call | solution.py:251
  396.3 12.8 %shard_map.185 = f32[384,640]{1,0:T(8,128)S(1)} custom-call(bf16[384,2560]{1,0:T(8,128)(2,1)S(1)} %pad_maximum_fusion.1.q_ref, bf16[384,1280]{1,0:T(8,128)(2,1)S(1)} %bitcast.55, bf16[384,2560]{1,0:T(8,128)(2,1)} %pad_maximum_fusion.2.attended_ref, bf16[2048,512]{1,0:T(8,128)(2,1)} %key_ref.15, bf16[2048,512]{1,0:T(8,128)(2,1)} %value_ref.15, ...), custom_call_target="tpu_custom_call" | custom-call | flops 3208642560 | bytes 6291456 | tf_op jit(solution)/shard_map/pallas_call | solution.py:251
  409.1 12.8 %shard_map.184 = f32[384,640]{1,0:T(8,128)S(1)} custom-call(bf16[384,2560]{1,0:T(8,128)(2,1)S(1)} %pad_maximum_fusion.1.q_ref, bf16[384,1280]{1,0:T(8,128)(2,1)S(1)} %bitcast.56, bf16[384,2560]{1,0:T(8,128)(2,1)} %pad_maximum_fusion.2.attended_ref, bf16[2048,512]{1,0:T(8,128)(2,1)} %key_ref.15, bf16[2048,512]{1,0:T(8,128)(2,1)} %value_ref.15, ...), custom_call_target="tpu_custom_call" | custom-call | flops 3208642560 | bytes 6291456 | tf_op jit(solution)/shard_map/pallas_call | solution.py:251
  426.5 5.7 %collective-permute-done.77 = bf16[1,2,1,2,24,1280]{5,4,3,2,1,0:T(8,128)(2,1)S(1)} collective-permute-done((bf16[1,2,1,2,24,1280]{5,4,3,2,1,0:T(8,128)(2,1)S(1)}, bf16[1,2,1,2,24,1280]{5,4,3,2,1,0:T(8,128)(2,1)S(1)}, u32[]{:S(2)}, u32[]{:S(2)}) %collective-permute-start.77) | collective-permute-done | bytes 245792 | tf_op jit(solution)/shard_map/ppermute | solution.py:32
  435.6 4.9 %collective-permute-done.78 = bf16[1,2,1,1,24,1280]{5,4,3,2,1,0:T(8,128)(2,1)S(1)} collective-permute-done((bf16[1,2,1,1,24,1280]{5,4,3,2,1,0:T(8,128)(2,1)S(1)}, bf16[1,2,1,1,24,1280]{5,4,3,2,1,0:T(8,128)(2,1)S(1)}, u32[]{:S(2)}, u32[]{:S(2)}) %collective-permute-start.78) | collective-permute-done | bytes 122912 | tf_op jit(solution)/shard_map/ppermute | solution.py:32
  450.7 5.0 %collective-permute-done.64 = bf16[1,1,1,1,24,1280]{5,4,3,2,1,0:T(8,128)(2,1)S(1)} collective-permute-done((bf16[1,1,1,1,24,1280]{5,4,3,2,1,0:T(8,128)(2,1)S(1)}, bf16[1,1,1,1,24,1280]{5,4,3,2,1,0:T(8,128)(2,1)S(1)}, u32[]{:S(2)}, u32[]{:S(2)}) %collective-permute-start.64) | collective-permute-done | bytes 61472 | tf_op jit(solution)/shard_map/ppermute | solution.py:32
  458.3 3.0 collective-permute-done.65
  461.5 4.5 collective-permute-done.82
  (393 shorter events, 138.6 us)
Async XLA Ops:
  2.8 102.1 %collective-permute-start = (f32[384]{0:T(512)S(1)}, f32[384]{0:T(512)}, u32[]{:S(2)}, u32[]{:S(2)}) collective-permute-start(f32[384]{0:T(512)S(1)} %fusion), channel_id=1, source_target_pairs={{0,1},{1,0},{2,3},{3,2},{4,5},{5,4},{6,7},{7,6},{8,9},{9,8},{10,11... | collective-permute-start | bytes 4616 | tf_op jit(solution)/shard_map/ppermute | solution.py:32
  9.7 13.9 %collective-permute-start.25 = (bf16[96,2560]{1,0:T(8,128)(2,1)S(1)}, bf16[96,2560]{1,0:T(8,128)(2,1)S(1)}, u32[]{:S(2)}, u32[]{:S(2)}) collective-permute-start(bf16[96,2560]{1,0:T(8,128)(2,1)S(1)} %dynamic_slice.245), channel_id=1, source_target_pairs={{0,1},{1,0},{2,3},{3,2},{4,5},{5,4},{6,7},{7,6},{8,9},{9,8},{10,11... | collective-permute-start | bytes 1474568 | tf_op jit(solution)/shard_map/ppermute | solution.py:32
  14.5 9.1 %collective-permute-start.28 = (bf16[96,512]{1,0:T(8,128)(2,1)S(1)}, bf16[96,512]{1,0:T(8,128)(2,1)S(1)}, u32[]{:S(2)}, u32[]{:S(2)}) collective-permute-start(bf16[96,512]{1,0:T(8,128)(2,1)S(1)} %collective-permute-done.27), channel_id=1, source_target_pairs={{0,2},{2,0},{4,6},{6,4},{8,10},{10,8},{12,14},{14,12},{16,18},{18,... | collective-permute-start | bytes 294920 | tf_op jit(solution)/shard_map/ppermute | solution.py:32
  88.6 12.2 %collective-permute-start.31 = (f32[384,40]{1,0:T(8,128)}, f32[384,40]{1,0:T(8,128)}, u32[]{:S(2)}, u32[]{:S(2)}) collective-permute-start(f32[384,40]{1,0:T(8,128)} %concatenate.172), channel_id=1, source_target_pairs={{0,2},{2,0},{4,6},{6,4},{8,10},{10,8},{12,14},{14,12},{16,18},{18,... | collective-permute-start | bytes 184328 | tf_op jit(solution)/shard_map/ppermute | solution.py:32
  99.6 50.0 %collective-permute-start.1 = (bf16[384,1728]{0,1:T(8,128)(2,1)}, bf16[384,1728]{0,1:T(8,128)(2,1)}, u32[]{:S(2)}, u32[]{:S(2)}) collective-permute-start(bf16[384,1728]{0,1:T(8,128)(2,1)} %get-tuple-element.129), channel_id=1, source_target_pairs={{0,1},{1,0},{2,3},{3,2},{4,5},{5,4},{6,7},{7,6},{8,9},{9,8},{10,11... | collective-permute-start | bytes 3981320 | tf_op jit(solution)/shard_map/ppermute | solution.py:32
  102.9 7.1 %collective-permute-start.32 = (f32[384,40]{1,0:T(8,128)S(1)}, f32[384,40]{1,0:T(8,128)S(1)}, u32[]{:S(2)}, u32[]{:S(2)}) collective-permute-start(f32[384,40]{1,0:T(8,128)S(1)} %pad_maximum_fusion.35), channel_id=1, source_target_pairs={{0,4},{2,6},{4,0},{6,2},{8,12},{10,14},{12,8},{14,10},{16,20},{18,... | collective-permute-start | bytes 184328 | tf_op jit(solution)/shard_map/ppermute | solution.py:32
  110.3 13.9 %collective-permute-start.33 = (f32[384,40]{1,0:T(8,128)S(1)}, f32[384,40]{1,0:T(8,128)S(1)}, u32[]{:S(2)}, u32[]{:S(2)}) collective-permute-start(f32[384,40]{1,0:T(8,128)S(1)} %pad_maximum_fusion.36), channel_id=1, source_target_pairs={{0,8},{2,10},{4,12},{6,14},{8,0},{10,2},{12,4},{14,6},{16,24},{18,... | collective-permute-start | bytes 184328 | tf_op jit(solution)/shard_map/ppermute | solution.py:32
  122.8 37.4 %collective-permute-start.3 = (bf16[384,1728]{0,1:T(8,128)(2,1)}, bf16[384,1728]{0,1:T(8,128)(2,1)}, u32[]{:S(2)}, u32[]{:S(2)}) collective-permute-start(bf16[384,1728]{0,1:T(8,128)(2,1)} %get-tuple-element.131), channel_id=1, source_target_pairs={{0,1},{1,0},{2,3},{3,2},{4,5},{5,4},{6,7},{7,6},{8,9},{9,8},{10,11... | collective-permute-start | bytes 3981320 | tf_op jit(solution)/shard_map/ppermute | solution.py:32
  124.4 10.1 %collective-permute-start.34 = (f32[384,40]{1,0:T(8,128)S(1)}, f32[384,40]{1,0:T(8,128)S(1)}, u32[]{:S(2)}, u32[]{:S(2)}) collective-permute-start(f32[384,40]{1,0:T(8,128)S(1)} %pad_maximum_fusion.37), channel_id=1, source_target_pairs={{0,16},{2,18},{4,20},{6,22},{8,24},{10,26},{12,28},{14,30},{16,0},... | collective-permute-start | bytes 184328 | tf_op jit(solution)/shard_map/ppermute | solution.py:32
  133.6 54.5 %collective-permute-start.2 = (bf16[384,1728]{0,1:T(8,128)(2,1)}, bf16[384,1728]{0,1:T(8,128)(2,1)}, u32[]{:S(2)}, u32[]{:S(2)}) collective-permute-start(bf16[384,1728]{0,1:T(8,128)(2,1)} %get-tuple-element.133), channel_id=1, source_target_pairs={{0,1},{1,0},{2,3},{3,2},{4,5},{5,4},{6,7},{7,6},{8,9},{9,8},{10,11... | collective-permute-start | bytes 3981320 | tf_op jit(solution)/shard_map/ppermute | solution.py:32
  148.9 85.3 %collective-permute-start.35 = (bf16[1,2,2,2,24,1280]{5,4,3,2,1,0:T(8,128)(2,1)}, bf16[1,2,2,2,24,1280]{5,4,3,2,1,0:T(8,128)(2,1)}, u32[]{:S(2)}, u32[]{:S(2)}) collective-permute-start(bf16[1,2,2,2,24,1280]{5,4,3,2,1,0:T(8,128)(2,1)} %dynamic-slice_convert_fusion.5), channel_id=1, source_target_pairs={{0,2},{2,0},{4,6},{6,4},{8,10},{10,8},{12,14},{14,12},{16,18},{18,... | collective-permute-start | bytes 1474568 | tf_op jit(solution)/shard_map/ppermute | solution.py:32
  148.9 88.1 %collective-permute-start.43 = (bf16[1,2,2,2,24,1280]{5,4,3,2,1,0:T(8,128)(2,1)S(1)}, bf16[1,2,2,2,24,1280]{5,4,3,2,1,0:T(8,128)(2,1)}, u32[]{:S(2)}, u32[]{:S(2)}) collective-permute-start(bf16[1,2,2,2,24,1280]{5,4,3,2,1,0:T(8,128)(2,1)S(1)} %dynamic-slice_convert_fusion.4), channel_id=1, source_target_pairs={{0,2},{2,0},{4,6},{6,4},{8,10},{10,8},{12,14},{14,12},{16,18},{18,... | collective-permute-start | bytes 1474568 | tf_op jit(solution)/shard_map/ppermute | solution.py:32
  214.3 25.6 %collective-permute-start.4 = (bf16[1,2,2,2,24,1280]{5,4,3,2,1,0:T(8,128)(2,1)}, bf16[1,2,2,2,24,1280]{5,4,3,2,1,0:T(8,128)(2,1)}, u32[]{:S(2)}, u32[]{:S(2)}) collective-permute-start(bf16[1,2,2,2,24,1280]{5,4,3,2,1,0:T(8,128)(2,1)} %dynamic-slice_convert_fusion.7), channel_id=1, source_target_pairs={{0,2},{2,0},{4,6},{6,4},{8,10},{10,8},{12,14},{14,12},{16,18},{18,... | collective-permute-start | bytes 1474568 | tf_op jit(solution)/shard_map/ppermute | solution.py:32
  214.3 27.3 %collective-permute-start.8 = (bf16[1,2,2,2,24,1280]{5,4,3,2,1,0:T(8,128)(2,1)S(1)}, bf16[1,2,2,2,24,1280]{5,4,3,2,1,0:T(8,128)(2,1)}, u32[]{:S(2)}, u32[]{:S(2)}) collective-permute-start(bf16[1,2,2,2,24,1280]{5,4,3,2,1,0:T(8,128)(2,1)S(1)} %dynamic-slice_convert_fusion.6), channel_id=1, source_target_pairs={{0,2},{2,0},{4,6},{6,4},{8,10},{10,8},{12,14},{14,12},{16,18},{18,... | collective-permute-start | bytes 1474568 | tf_op jit(solution)/shard_map/ppermute | solution.py:32
  235.4 8.1 %collective-permute-start.36 = (bf16[1,1,2,2,24,1280]{5,4,3,2,1,0:T(8,128)(2,1)S(1)}, bf16[1,1,2,2,24,1280]{5,4,3,2,1,0:T(8,128)(2,1)S(1)}, u32[]{:S(2)}, u32[]{:S(2)}) collective-permute-start(bf16[1,1,2,2,24,1280]{5,4,3,2,1,0:T(8,128)(2,1)S(1)} %dynamic-slice_convert_fusion.13), channel_id=1, source_target_pairs={{0,4},{2,6},{4,0},{6,2},{8,12},{10,14},{12,8},{14,10},{16,20},{18,... | collective-permute-start | bytes 737288 | tf_op jit(solution)/shard_map/ppermute | solution.py:32
  238.2 8.6 %collective-permute-start.44 = (bf16[1,2,1,2,24,1280]{5,4,3,2,1,0:T(8,128)(2,1)S(1)}, bf16[1,2,1,2,24,1280]{5,4,3,2,1,0:T(8,128)(2,1)S(1)}, u32[]{:S(2)}, u32[]{:S(2)}) collective-permute-start(bf16[1,2,1,2,24,1280]{5,4,3,2,1,0:T(8,128)(2,1)S(1)} %dynamic-slice_convert_fusion.12), channel_id=1, source_target_pairs={{0,8},{2,10},{4,12},{6,14},{8,0},{10,2},{12,4},{14,6},{16,24},{18,... | collective-permute-start | bytes 737288 | tf_op jit(solution)/shard_map/ppermute | solution.py:32
  241.0 8.6 %collective-permute-start.5 = (bf16[1,1,2,2,24,1280]{5,4,3,2,1,0:T(8,128)(2,1)S(1)}, bf16[1,1,2,2,24,1280]{5,4,3,2,1,0:T(8,128)(2,1)S(1)}, u32[]{:S(2)}, u32[]{:S(2)}) collective-permute-start(bf16[1,1,2,2,24,1280]{5,4,3,2,1,0:T(8,128)(2,1)S(1)} %dynamic-slice_convert_fusion.15), channel_id=1, source_target_pairs={{0,4},{2,6},{4,0},{6,2},{8,12},{10,14},{12,8},{14,10},{16,20},{18,... | collective-permute-start | bytes 737288 | tf_op jit(solution)/shard_map/ppermute | solution.py:32
  242.8 12.0 %collective-permute-start.9 = (bf16[1,2,1,2,24,1280]{5,4,3,2,1,0:T(8,128)(2,1)S(1)}, bf16[1,2,1,2,24,1280]{5,4,3,2,1,0:T(8,128)(2,1)S(1)}, u32[]{:S(2)}, u32[]{:S(2)}) collective-permute-start(bf16[1,2,1,2,24,1280]{5,4,3,2,1,0:T(8,128)(2,1)S(1)} %dynamic-slice_convert_fusion.14), channel_id=1, source_target_pairs={{0,8},{2,10},{4,12},{6,14},{8,0},{10,2},{12,4},{14,6},{16,24},{18,... | collective-permute-start | bytes 737288 | tf_op jit(solution)/shard_map/ppermute | solution.py:32
  243.5 15.2 %collective-permute-start.37 = (bf16[1,1,1,2,24,1280]{5,4,3,2,1,0:T(8,128)(2,1)S(1)}, bf16[1,1,1,2,24,1280]{5,4,3,2,1,0:T(8,128)(2,1)S(1)}, u32[]{:S(2)}, u32[]{:S(2)}) collective-permute-start(bf16[1,1,1,2,24,1280]{5,4,3,2,1,0:T(8,128)(2,1)S(1)} %dynamic-slice_convert_fusion.21), channel_id=1, source_target_pairs={{0,8},{2,10},{4,12},{6,14},{8,0},{10,2},{12,4},{14,6},{16,24},{18,... | collective-permute-start | bytes 368648 | tf_op jit(solution)/shard_map/ppermute | solution.py:32
  246.9 13.7 %collective-permute-start.45 = (bf16[1,2,1,1,24,1280]{5,4,3,2,1,0:T(8,128)(2,1)S(1)}, bf16[1,2,1,1,24,1280]{5,4,3,2,1,0:T(8,128)(2,1)S(1)}, u32[]{:S(2)}, u32[]{:S(2)}) collective-permute-start(bf16[1,2,1,1,24,1280]{5,4,3,2,1,0:T(8,128)(2,1)S(1)} %dynamic-slice_convert_fusion.20), channel_id=1, source_target_pairs={{0,16},{2,18},{4,20},{6,22},{8,24},{10,26},{12,28},{14,30},{16,0},... | collective-permute-start | bytes 368648 | tf_op jit(solution)/shard_map/ppermute | solution.py:32
  249.7 17.8 %collective-permute-start.6 = (bf16[1,1,1,2,24,1280]{5,4,3,2,1,0:T(8,128)(2,1)S(1)}, bf16[1,1,1,2,24,1280]{5,4,3,2,1,0:T(8,128)(2,1)S(1)}, u32[]{:S(2)}, u32[]{:S(2)}) collective-permute-start(bf16[1,1,1,2,24,1280]{5,4,3,2,1,0:T(8,128)(2,1)S(1)} %dynamic-slice_convert_fusion.23), channel_id=1, source_target_pairs={{0,8},{2,10},{4,12},{6,14},{8,0},{10,2},{12,4},{14,6},{16,24},{18,... | collective-permute-start | bytes 368648 | tf_op jit(solution)/shard_map/ppermute | solution.py:32
  254.8 15.7 %collective-permute-start.10 = (bf16[1,2,1,1,24,1280]{5,4,3,2,1,0:T(8,128)(2,1)S(1)}, bf16[1,2,1,1,24,1280]{5,4,3,2,1,0:T(8,128)(2,1)S(1)}, u32[]{:S(2)}, u32[]{:S(2)}) collective-permute-start(bf16[1,2,1,1,24,1280]{5,4,3,2,1,0:T(8,128)(2,1)S(1)} %dynamic-slice_convert_fusion.22), channel_id=1, source_target_pairs={{0,16},{2,18},{4,20},{6,22},{8,24},{10,26},{12,28},{14,30},{16,0},... | collective-permute-start | bytes 368648 | tf_op jit(solution)/shard_map/ppermute | solution.py:32
  258.8 7.5 %collective-permute-start.38 = (bf16[1,1,1,1,24,1280]{5,4,3,2,1,0:T(8,128)(2,1)S(1)}, bf16[1,1,1,1,24,1280]{5,4,3,2,1,0:T(8,128)(2,1)S(1)}, u32[]{:S(2)}, u32[]{:S(2)}) collective-permute-start(bf16[1,1,1,1,24,1280]{5,4,3,2,1,0:T(8,128)(2,1)S(1)} %dynamic-slice_convert_fusion.29), channel_id=1, source_target_pairs={{0,16},{2,18},{4,20},{6,22},{8,24},{10,26},{12,28},{14,30},{16,0},... | collective-permute-start | bytes 184328 | tf_op jit(solution)/shard_map/ppermute | solution.py:32
  266.4 7.3 %collective-permute-start.47 = (bf16[1,1,1,1,24,1280]{5,4,3,2,1,0:T(8,128)(2,1)S(1)}, bf16[1,1,1,1,24,1280]{5,4,3,2,1,0:T(8,128)(2,1)S(1)}, u32[]{:S(2)}, u32[]{:S(2)}) collective-permute-start(bf16[1,1,1,1,24,1280]{5,4,3,2,1,0:T(8,128)(2,1)S(1)} %add_convert_fusion.5), channel_id=1, source_target_pairs={{0,4},{2,6},{4,0},{6,2},{8,12},{10,14},{12,8},{14,10},{16,20},{18,... | collective-permute-start | bytes 184328 | tf_op jit(solution)/shard_map/ppermute | solution.py:32
  271.6 23.6 %collective-permute-start.40 = (bf16[1,1,1,2,24,1280]{5,4,3,2,1,0:T(8,128)(2,1)S(1)}, bf16[1,1,1,2,24,1280]{5,4,3,2,1,0:T(8,128)(2,1)S(1)}, u32[]{:S(2)}, u32[]{:S(2)}) collective-permute-start(bf16[1,1,1,2,24,1280]{5,4,3,2,1,0:T(8,128)(2,1)S(1)} %pad_maximum_fusion.40), channel_id=1, source_target_pairs={{0,8},{2,10},{4,12},{6,14},{8,0},{10,2},{12,4},{14,6},{16,24},{18,... | collective-permute-start | bytes 368648 | tf_op jit(solution)/shard_map/ppermute | solution.py:32
  283.8 10.7 %collective-permute-start.13 = (bf16[1,1,1,1,24,1280]{5,4,3,2,1,0:T(8,128)(2,1)S(1)}, bf16[1,1,1,1,24,1280]{5,4,3,2,1,0:T(8,128)(2,1)S(1)}, u32[]{:S(2)}, u32[]{:S(2)}) collective-permute-start(bf16[1,1,1,1,24,1280]{5,4,3,2,1,0:T(8,128)(2,1)S(1)} %get-tuple-element.127), channel_id=1, source_target_pairs={{0,16},{2,18},{4,20},{6,22},{8,24},{10,26},{12,28},{14,30},{16,0},... | collective-permute-start | bytes 184328 | tf_op jit(solution)/shard_map/ppermute | solution.py:32
  286.0 8.6 %collective-permute-start.17 = (bf16[1,1,1,1,24,1280]{5,4,3,2,1,0:T(8,128)(2,1)S(1)}, bf16[1,1,1,1,24,1280]{5,4,3,2,1,0:T(8,128)(2,1)S(1)}, u32[]{:S(2)}, u32[]{:S(2)}) collective-permute-start(bf16[1,1,1,1,24,1280]{5,4,3,2,1,0:T(8,128)(2,1)S(1)} %get-tuple-element.128), channel_id=1, source_target_pairs={{0,4},{2,6},{4,0},{6,2},{8,12},{10,14},{12,8},{14,10},{16,20},{18,... | collective-permute-start | bytes 184328 | tf_op jit(solution)/shard_map/ppermute | solution.py:32
  288.8 10.1 %collective-permute-start.48 = (bf16[1,2,1,1,24,1280]{5,4,3,2,1,0:T(8,128)(2,1)S(1)}, bf16[1,2,1,1,24,1280]{5,4,3,2,1,0:T(8,128)(2,1)S(1)}, u32[]{:S(2)}, u32[]{:S(2)}) collective-permute-start(bf16[1,2,1,1,24,1280]{5,4,3,2,1,0:T(8,128)(2,1)S(1)} %pad_maximum_fusion.41), channel_id=1, source_target_pairs={{0,16},{2,18},{4,20},{6,22},{8,24},{10,26},{12,28},{14,30},{16,0},... | collective-permute-start | bytes 368648 | tf_op jit(solution)/shard_map/ppermute | solution.py:32
  294.7 7.6 %collective-permute-start.14 = (bf16[1,1,1,2,24,1280]{5,4,3,2,1,0:T(8,128)(2,1)S(1)}, bf16[1,1,1,2,24,1280]{5,4,3,2,1,0:T(8,128)(2,1)S(1)}, u32[]{:S(2)}, u32[]{:S(2)}) collective-permute-start(bf16[1,1,1,2,24,1280]{5,4,3,2,1,0:T(8,128)(2,1)S(1)} %pad_maximum_fusion.38), channel_id=1, source_target_pairs={{0,8},{2,10},{4,12},{6,14},{8,0},{10,2},{12,4},{14,6},{16,24},{18,... | collective-permute-start | bytes 368648 | tf_op jit(solution)/shard_map/ppermute | solution.py:32
  295.3 10.0 %collective-permute-start.41 = (bf16[1,1,2,2,24,1280]{5,4,3,2,1,0:T(8,128)(2,1)S(1)}, bf16[1,1,2,2,24,1280]{5,4,3,2,1,0:T(8,128)(2,1)S(1)}, u32[]{:S(2)}, u32[]{:S(2)}) collective-permute-start(bf16[1,1,2,2,24,1280]{5,4,3,2,1,0:T(8,128)(2,1)S(1)} %pad_maximum_fusion.26), channel_id=1, source_target_pairs={{0,4},{2,6},{4,0},{6,2},{8,12},{10,14},{12,8},{14,10},{16,20},{18,... | collective-permute-start | bytes 737288 | tf_op jit(solution)/shard_map/ppermute | solution.py:32
  298.9 9.0 %collective-permute-start.49 = (bf16[1,2,1,2,24,1280]{5,4,3,2,1,0:T(8,128)(2,1)S(1)}, bf16[1,2,1,2,24,1280]{5,4,3,2,1,0:T(8,128)(2,1)S(1)}, u32[]{:S(2)}, u32[]{:S(2)}) collective-permute-start(bf16[1,2,1,2,24,1280]{5,4,3,2,1,0:T(8,128)(2,1)S(1)} %pad_maximum_fusion.27), channel_id=1, source_target_pairs={{0,8},{2,10},{4,12},{6,14},{8,0},{10,2},{12,4},{14,6},{16,24},{18,... | collective-permute-start | bytes 737288 | tf_op jit(solution)/shard_map/ppermute | solution.py:32
  301.1 9.9 %collective-permute-start.19 = (bf16[1,2,1,2,24,1280]{5,4,3,2,1,0:T(8,128)(2,1)S(1)}, bf16[1,2,1,2,24,1280]{5,4,3,2,1,0:T(8,128)(2,1)S(1)}, u32[]{:S(2)}, u32[]{:S(2)}) collective-permute-start(bf16[1,2,1,2,24,1280]{5,4,3,2,1,0:T(8,128)(2,1)S(1)} %pad_maximum_fusion.25), channel_id=1, source_target_pairs={{0,8},{2,10},{4,12},{6,14},{8,0},{10,2},{12,4},{14,6},{16,24},{18,... | collective-permute-start | bytes 737288 | tf_op jit(solution)/shard_map/ppermute | solution.py:32
  302.4 8.8 %collective-permute-start.15 = (bf16[1,1,2,2,24,1280]{5,4,3,2,1,0:T(8,128)(2,1)S(1)}, bf16[1,1,2,2,24,1280]{5,4,3,2,1,0:T(8,128)(2,1)S(1)}, u32[]{:S(2)}, u32[]{:S(2)}) collective-permute-start(bf16[1,1,2,2,24,1280]{5,4,3,2,1,0:T(8,128)(2,1)S(1)} %pad_maximum_fusion.24), channel_id=1, source_target_pairs={{0,4},{2,6},{4,0},{6,2},{8,12},{10,14},{12,8},{14,10},{16,20},{18,... | collective-permute-start | bytes 737288 | tf_op jit(solution)/shard_map/ppermute | solution.py:32
  314.4 9.1 %collective-permute-start.51 = (bf16[384,320]{1,0:T(8,128)(2,1)S(1)}, bf16[384,320]{1,0:T(8,128)(2,1)S(1)}, u32[]{:S(2)}, u32[]{:S(2)}) collective-permute-start(bf16[384,320]{1,0:T(8,128)(2,1)S(1)} %fusion.8), channel_id=1, source_target_pairs={{0,1},{1,0},{2,3},{3,2},{4,5},{5,4},{6,7},{7,6},{8,9},{9,8},{10,11... | collective-permute-start | bytes 737288 | tf_op jit(solution)/shard_map/ppermute | solution.py:32
  328.1 8.0 %collective-permute-start.69 = (bf16[1,2,1,2,24,1280]{5,4,3,2,1,0:T(8,128)(2,1)S(1)}, bf16[1,2,1,2,24,1280]{5,4,3,2,1,0:T(8,128)(2,1)S(1)}, u32[]{:S(2)}, u32[]{:S(2)}) collective-permute-start(bf16[1,2,1,2,24,1280]{5,4,3,2,1,0:T(8,128)(2,1)S(1)} %dynamic-slice_convert_fusion.9), channel_id=1, source_target_pairs={{0,8},{2,10},{4,12},{6,14},{8,0},{10,2},{12,4},{14,6},{16,24},{18,... | collective-permute-start | bytes 737288 | tf_op jit(solution)/shard_map/ppermute | solution.py:32
  328.3 8.0 %collective-permute-start.53 = (bf16[1,1,2,2,24,1280]{5,4,3,2,1,0:T(8,128)(2,1)S(1)}, bf16[1,1,2,2,24,1280]{5,4,3,2,1,0:T(8,128)(2,1)S(1)}, u32[]{:S(2)}, u32[]{:S(2)}) collective-permute-start(bf16[1,1,2,2,24,1280]{5,4,3,2,1,0:T(8,128)(2,1)S(1)} %dynamic-slice_convert_fusion.11), channel_id=1, source_target_pairs={{0,4},{2,6},{4,0},{6,2},{8,12},{10,14},{12,8},{14,10},{16,20},{18,... | collective-permute-start | bytes 737288 | tf_op jit(solution)/shard_map/ppermute | solution.py:32
  336.1 8.0 %collective-permute-start.70 = (bf16[1,2,1,1,24,1280]{5,4,3,2,1,0:T(8,128)(2,1)S(1)}, bf16[1,2,1,1,24,1280]{5,4,3,2,1,0:T(8,128)(2,1)S(1)}, u32[]{:S(2)}, u32[]{:S(2)}) collective-permute-start(bf16[1,2,1,1,24,1280]{5,4,3,2,1,0:T(8,128)(2,1)S(1)} %dynamic-slice_convert_fusion.17), channel_id=1, source_target_pairs={{0,16},{2,18},{4,20},{6,22},{8,24},{10,26},{12,28},{14,30},{16,0},... | collective-permute-start | bytes 368648 | tf_op jit(solution)/shard_map/ppermute | solution.py:32
  336.3 9.0 %collective-permute-start.54 = (bf16[1,1,1,2,24,1280]{5,4,3,2,1,0:T(8,128)(2,1)S(1)}, bf16[1,1,1,2,24,1280]{5,4,3,2,1,0:T(8,128)(2,1)S(1)}, u32[]{:S(2)}, u32[]{:S(2)}) collective-permute-start(bf16[1,1,1,2,24,1280]{5,4,3,2,1,0:T(8,128)(2,1)S(1)} %dynamic-slice_convert_fusion.19), channel_id=1, source_target_pairs={{0,8},{2,10},{4,12},{6,14},{8,0},{10,2},{12,4},{14,6},{16,24},{18,... | collective-permute-start | bytes 368648 | tf_op jit(solution)/shard_map/ppermute | solution.py:32
  352.8 7.8 %collective-permute-start.73 = (bf16[1,2,1,1,24,1280]{5,4,3,2,1,0:T(8,128)(2,1)S(1)}, bf16[1,2,1,1,24,1280]{5,4,3,2,1,0:T(8,128)(2,1)S(1)}, u32[]{:S(2)}, u32[]{:S(2)}) collective-permute-start(bf16[1,2,1,1,24,1280]{5,4,3,2,1,0:T(8,128)(2,1)S(1)} %pad_maximum_fusion.44), channel_id=1, source_target_pairs={{0,16},{2,18},{4,20},{6,22},{8,24},{10,26},{12,28},{14,30},{16,0},... | collective-permute-start | bytes 368648 | tf_op jit(solution)/shard_map/ppermute | solution.py:32
  360.7 7.3 %collective-permute-start.74 = (bf16[1,2,1,2,24,1280]{5,4,3,2,1,0:T(8,128)(2,1)S(1)}, bf16[1,2,1,2,24,1280]{5,4,3,2,1,0:T(8,128)(2,1)S(1)}, u32[]{:S(2)}, u32[]{:S(2)}) collective-permute-start(bf16[1,2,1,2,24,1280]{5,4,3,2,1,0:T(8,128)(2,1)S(1)} %pad_maximum_fusion.30), channel_id=1, source_target_pairs={{0,8},{2,10},{4,12},{6,14},{8,0},{10,2},{12,4},{14,6},{16,24},{18,... | collective-permute-start | bytes 737288 | tf_op jit(solution)/shard_map/ppermute | solution.py:32
  369.0 27.1 %collective-permute-start.59 = (bf16[1,2,2,2,24,1280]{5,4,3,2,1,0:T(8,128)(2,1)S(1)}, bf16[1,2,2,2,24,1280]{5,4,3,2,1,0:T(8,128)(2,1)S(1)}, u32[]{:S(2)}, u32[]{:S(2)}) collective-permute-start(bf16[1,2,2,2,24,1280]{5,4,3,2,1,0:T(8,128)(2,1)S(1)} %pad_maximum_fusion.19), channel_id=1, source_target_pairs={{0,2},{2,0},{4,6},{6,4},{8,10},{10,8},{12,14},{14,12},{16,18},{18,... | collective-permute-start | bytes 1474568 | tf_op jit(solution)/shard_map/ppermute | solution.py:32
  424.1 8.1 %collective-permute-start.77 = (bf16[1,2,1,2,24,1280]{5,4,3,2,1,0:T(8,128)(2,1)S(1)}, bf16[1,2,1,2,24,1280]{5,4,3,2,1,0:T(8,128)(2,1)S(1)}, u32[]{:S(2)}, u32[]{:S(2)}) collective-permute-start(bf16[1,2,1,2,24,1280]{5,4,3,2,1,0:T(8,128)(2,1)S(1)} %dynamic-slice_convert_fusion.8), channel_id=1, source_target_pairs={{0,8},{2,10},{4,12},{6,14},{8,0},{10,2},{12,4},{14,6},{16,24},{18,... | collective-permute-start | bytes 737288 | tf_op jit(solution)/shard_map/ppermute | solution.py:32
  425.2 8.4 %collective-permute-start.61 = (bf16[1,1,2,2,24,1280]{5,4,3,2,1,0:T(8,128)(2,1)S(1)}, bf16[1,1,2,2,24,1280]{5,4,3,2,1,0:T(8,128)(2,1)S(1)}, u32[]{:S(2)}, u32[]{:S(2)}) collective-permute-start(bf16[1,1,2,2,24,1280]{5,4,3,2,1,0:T(8,128)(2,1)S(1)} %dynamic-slice_convert_fusion.10), channel_id=1, source_target_pairs={{0,4},{2,6},{4,0},{6,2},{8,12},{10,14},{12,8},{14,10},{16,20},{18,... | collective-permute-start | bytes 737288 | tf_op jit(solution)/shard_map/ppermute | solution.py:32
  432.3 8.2 %collective-permute-start.78 = (bf16[1,2,1,1,24,1280]{5,4,3,2,1,0:T(8,128)(2,1)S(1)}, bf16[1,2,1,1,24,1280]{5,4,3,2,1,0:T(8,128)(2,1)S(1)}, u32[]{:S(2)}, u32[]{:S(2)}) collective-permute-start(bf16[1,2,1,1,24,1280]{5,4,3,2,1,0:T(8,128)(2,1)S(1)} %dynamic-slice_convert_fusion.16), channel_id=1, source_target_pairs={{0,16},{2,18},{4,20},{6,22},{8,24},{10,26},{12,28},{14,30},{16,0},... | collective-permute-start | bytes 368648 | tf_op jit(solution)/shard_map/ppermute | solution.py:32
  433.7 8.3 %collective-permute-start.62 = (bf16[1,1,1,2,24,1280]{5,4,3,2,1,0:T(8,128)(2,1)S(1)}, bf16[1,1,1,2,24,1280]{5,4,3,2,1,0:T(8,128)(2,1)S(1)}, u32[]{:S(2)}, u32[]{:S(2)}) collective-permute-start(bf16[1,1,1,2,24,1280]{5,4,3,2,1,0:T(8,128)(2,1)S(1)} %dynamic-slice_convert_fusion.18), channel_id=1, source_target_pairs={{0,8},{2,10},{4,12},{6,14},{8,0},{10,2},{12,4},{14,6},{16,24},{18,... | collective-permute-start | bytes 368648 | tf_op jit(solution)/shard_map/ppermute | solution.py:32
  447.6 8.1 %collective-permute-start.64 = (bf16[1,1,1,1,24,1280]{5,4,3,2,1,0:T(8,128)(2,1)S(1)}, bf16[1,1,1,1,24,1280]{5,4,3,2,1,0:T(8,128)(2,1)S(1)}, u32[]{:S(2)}, u32[]{:S(2)}) collective-permute-start(bf16[1,1,1,1,24,1280]{5,4,3,2,1,0:T(8,128)(2,1)S(1)} %add_convert_fusion.3), channel_id=1, source_target_pairs={{0,16},{2,18},{4,20},{6,22},{8,24},{10,26},{12,28},{14,30},{16,0},... | collective-permute-start | bytes 184328 | tf_op jit(solution)/shard_map/ppermute | solution.py:32
  449.2 9.0 %collective-permute-start.81 = (bf16[1,2,1,1,24,1280]{5,4,3,2,1,0:T(8,128)(2,1)S(1)}, bf16[1,2,1,1,24,1280]{5,4,3,2,1,0:T(8,128)(2,1)S(1)}, u32[]{:S(2)}, u32[]{:S(2)}) collective-permute-start(bf16[1,2,1,1,24,1280]{5,4,3,2,1,0:T(8,128)(2,1)S(1)} %pad_maximum_fusion.45), channel_id=1, source_target_pairs={{0,16},{2,18},{4,20},{6,22},{8,24},{10,26},{12,28},{14,30},{16,0},... | collective-permute-start | bytes 368648 | tf_op jit(solution)/shard_map/ppermute | solution.py:32
  458.2 7.8 %collective-permute-start.82 = (bf16[1,2,1,2,24,1280]{5,4,3,2,1,0:T(8,128)(2,1)S(1)}, bf16[1,2,1,2,24,1280]{5,4,3,2,1,0:T(8,128)(2,1)S(1)}, u32[]{:S(2)}, u32[]{:S(2)}) collective-permute-start(bf16[1,2,1,2,24,1280]{5,4,3,2,1,0:T(8,128)(2,1)S(1)} %pad_maximum_fusion.31), channel_id=1, source_target_pairs={{0,8},{2,10},{4,12},{6,14},{8,0},{10,2},{12,4},{14,6},{16,24},{18,... | collective-permute-start | bytes 737288 | tf_op jit(solution)/shard_map/ppermute | solution.py:32
  (73 other events, 723.2 us)

commit v2 on v1

--- a/solution.py
+++ b/solution.py
@@ -27,9 +27,9 @@
     )
 
 
-def swapped(array, axis, bit):
+def swapped(array, axis, mask):
     size = lax.axis_size(axis)
-    return lax.ppermute(array, axis, [(i, i ^ (1 << bit)) for i in range(size)])
+    return lax.ppermute(array, axis, [(i, i ^ mask) for i in range(size)])
 
 
 def wide_bits():
@@ -45,23 +45,50 @@
     return array.reshape((2,) * wide_bits() + (array.shape[0] // count, array.shape[1]))
 
 
-def scatter_sum(cube, order):
-    for k in order:
-        bit = bit_of(k)
-        sent = lax.dynamic_slice_in_dim(cube, 1 - bit, 1, k).astype(jnp.bfloat16)
-        kept = lax.dynamic_slice_in_dim(cube, bit, 1, k).astype(jnp.float32)
-        cube = kept + swapped(sent, "wide", k).astype(jnp.float32)
+def masks(stage):
+    found = [0]
+    for k in stage:
+        found += [mask | (1 << k) for mask in found]
+    return found
+
+
+def part_for(cube, stage, mask):
+    for k in stage:
+        cube = lax.dynamic_slice_in_dim(cube, bit_of(k) ^ ((mask >> k) & 1), 1, k)
+    return cube
+
+
+def scatter_sum(cube, stages):
+    for stage in stages:
+        low = cube.astype(jnp.bfloat16)
+        total = part_for(cube, stage, 0).astype(jnp.float32)
+        for mask in masks(stage)[1:]:
+            got = swapped(part_for(low, stage, mask), "wide", mask)
+            total = total + got.astype(jnp.float32)
+        cube = total
     return cube.reshape(cube.shape[-2:])
 
 
-def gathered(chunk, order):
+def gathered(chunk, stages):
     cube = chunk.reshape((1,) * wide_bits() + chunk.shape)
-    for k in reversed(order):
-        other = swapped(cube, "wide", k)
-        first = bit_of(k) == 0
-        cube = jnp.concatenate(
-            [jnp.where(first, cube, other), jnp.where(first, other, cube)], axis=k
-        )
+    for stage in reversed(stages):
+        held = {0: cube}
+        for mask in masks(stage)[1:]:
+            held[mask] = swapped(cube, "wide", mask)
+        for k in stage:
+            first = bit_of(k) == 0
+            held = {
+                mask: jnp.concatenate(
+                    [
+                        jnp.where(first, held[mask], held[mask | (1 << k)]),
+                        jnp.where(first, held[mask | (1 << k)], held[mask]),
+                    ],
+                    axis=k,
+                )
+                for mask in held
+                if not mask & (1 << k)
+            }
+        cube = held[0]
     return cube.reshape(-1, cube.shape[-1])
 
 
@@ -74,26 +101,29 @@
 
 def doubled(value, combine):
     for k in range(wide_bits()):
-        value = combine(value, swapped(value, "wide", k))
+        value = combine(value, swapped(value, "wide", 1 << k))
     return value
 
 
 def orders():
-    bits = wide_bits()
-    plain = list(range(bits))
-    return (plain, plain[:1] + plain[2:] + plain[1:2])
+    core, side, line = (0,), (1,), tuple(range(2, wide_bits()))
+    return ([core, side, line], [core, line, side])
 
 
 def narrow_sum(part):
     if lax.axis_size("narrow") == 2:
-        return part + swapped(part, "narrow", 0)
+        return part + swapped(part, "narrow", 1)
     return lax.psum(part, "narrow")
 
 
-def narrow_total(part):
+def narrow_total(part, low):
     if lax.axis_size("narrow") == 2:
-        return part + swapped(part.astype(jnp.bfloat16), "narrow", 0).astype(jnp.float32)
+        return part + swapped(low, "narrow", 1).astype(jnp.float32)
     return lax.psum(part, "narrow")
+
+
+def after(arrays, *others):
+    return lax.optimization_barrier((tuple(arrays), others))[0]
 
 
 def to_heads(rows):
@@ -105,8 +135,8 @@
     bit = bit_of(0)
     kept = lax.dynamic_slice_in_dim(rows, place * half, half, 1)
     sent = lax.dynamic_slice(rows, (bit * count, (1 - place) * half), (count, half))
-    got = swapped(sent, "narrow", 0)
-    other = swapped(got, "wide", 0)
+    got = swapped(sent, "narrow", 1)
+    other = swapped(got, "wide", 1)
     first = bit == 0
     far = jnp.concatenate([jnp.where(first, got, other), jnp.where(first, other, got)], axis=0)
     low = place == 0
@@ -153,10 +183,10 @@
 
 
 def forward_kernel(
-    base, q_ref, key_ref, value_ref, own_key_ref, own_value_ref,
+    per_group, base, q_ref, key_ref, value_ref, own_key_ref, own_value_ref,
     from_ref, own_ref, out_ref, top_ref, total_ref,
 ):
-    head = pl.program_id(0)
+    head = pl.program_id(0) * per_group + pl.program_id(1)
 
     @pl.when(head == 0)
     def _():
@@ -182,10 +212,10 @@
 
 
 def backward_kernel(
-    first_head, base, scale, q_ref, grad_ref, attended_ref, key_ref, value_ref,
+    first_group, per_group, base, scale, q_ref, grad_ref, attended_ref, key_ref, value_ref,
     own_key_ref, own_value_ref, from_ref, own_ref, top_ref, inverse_ref, out_ref,
 ):
-    head = first_head + pl.program_id(0)
+    head = (first_group + pl.program_id(0)) * per_group + pl.program_id(1)
     cached, own = raw_scores(q_ref[...], key_ref, own_key_ref, from_ref, own_ref)
     top = pick_lane(top_ref, head)
     inverse = pick_lane(inverse_ref, head)
@@ -205,58 +235,57 @@
     out_ref[...] = (out * (inverse * scale)).astype(out_ref.dtype)
 
 
-def blocks(tokens, cached, padded, group, first):
-    head = pl.BlockSpec((tokens, HEAD_DIM), lambda p: (0, first + p))
-    rows = pl.BlockSpec((cached, HEAD_DIM), lambda p: (0, group))
-    own = pl.BlockSpec((padded, HEAD_DIM), lambda p: (0, group))
-    bound = pl.BlockSpec((tokens, 1), lambda p: (0, 0))
-    stat = pl.BlockSpec((tokens, HEAD_DIM), lambda p: (0, 0))
-    return (head, rows, own, bound, stat)
-
-
-def forward_group(group, per_group, base, queries, keys, values, own_keys, own_values, bounds):
+def blocks(tokens, cached, padded, per_group, first):
+    head = pl.BlockSpec((tokens, HEAD_DIM), lambda g, p: (0, (first + g) * per_group + p))
+    rows = pl.BlockSpec((cached, HEAD_DIM), lambda g, p: (0, first + g))
+    own = pl.BlockSpec((padded, HEAD_DIM), lambda g, p: (0, first + g))
+    bound = pl.BlockSpec((tokens, 1), lambda g, p: (0, 0))
+    stat = pl.BlockSpec((tokens, HEAD_DIM), lambda g, p: (0, 0))
+    here = pl.BlockSpec((tokens, HEAD_DIM), lambda g, p: (0, g * per_group + p))
+    return (head, rows, own, bound, stat, here)
+
+
+def forward(
+    first, groups, per_group, base, queries, keys, values, own_keys, own_values, bounds
+):
     tokens = queries.shape[0]
     cached, padded = keys.shape[0], own_keys.shape[0]
-    head, rows, own, bound, stat = blocks(tokens, cached, padded, group, group * per_group)
-    out = pl.BlockSpec((tokens, HEAD_DIM), lambda p: (0, p))
-    work = per_group * tokens * (cached + padded)
+    head, rows, own, bound, stat, here = blocks(tokens, cached, padded, per_group, first)
+    work = groups * per_group * tokens * (cached + padded)
     return pl.pallas_call(
-        functools.partial(forward_kernel, base),
-        grid=(per_group,),
+        functools.partial(forward_kernel, per_group, base),
+        grid=(groups, per_group),
         in_specs=[head, rows, rows, own, own, bound, bound],
-        out_specs=[out, stat, stat],
+        out_specs=[here, stat, stat],
         out_shape=[
-            jax.ShapeDtypeStruct((tokens, per_group * HEAD_DIM), jnp.float32),
+            jax.ShapeDtypeStruct((tokens, groups * per_group * HEAD_DIM), jnp.float32),
             jax.ShapeDtypeStruct((tokens, HEAD_DIM), jnp.float32),
             jax.ShapeDtypeStruct((tokens, HEAD_DIM), jnp.float32),
         ],
         compiler_params=pltpu.CompilerParams(vmem_limit_bytes=40 << 20),
         cost_estimate=pl.CostEstimate(
-            flops=4 * HEAD_DIM * work, bytes_accessed=6 << 20, transcendentals=work
+            flops=16 * HEAD_DIM * work, bytes_accessed=20 << 20, transcendentals=work
         ),
     )(queries, keys, values, own_keys, own_values, *bounds)
 
 
-def backward_group(
-    group, per_group, base, scale, queries, grads, attended, keys, values,
-    own_keys, own_values, bounds, top, inverse, shift,
+def backward(
+    first, groups, per_group, base, scale, queries, grads, attended, keys, values,
+    own_keys, own_values, bounds, top, inverse,
 ):
     tokens = queries.shape[0]
     cached, padded = keys.shape[0], own_keys.shape[0]
-    first = group * per_group
-    head, rows, own, bound, stat = blocks(tokens, cached, padded, group, first)
-    grad = pl.BlockSpec((tokens, HEAD_DIM), lambda p: (0, first - shift + p))
-    out = pl.BlockSpec((tokens, HEAD_DIM), lambda p: (0, p))
-    work = per_group * tokens * (cached + padded)
+    head, rows, own, bound, stat, here = blocks(tokens, cached, padded, per_group, first)
+    work = groups * per_group * tokens * (cached + padded)
     return pl.pallas_call(
-        functools.partial(backward_kernel, first, base, scale),
-        grid=(per_group,),
-        in_specs=[head, grad, head, rows, rows, own, own, bound, bound, stat, stat],
-        out_specs=out,
-        out_shape=jax.ShapeDtypeStruct((tokens, per_group * HEAD_DIM), jnp.float32),
+        functools.partial(backward_kernel, first, per_group, base, scale),
+        grid=(groups, per_group),
+        in_specs=[head, here, head, rows, rows, own, own, bound, bound, stat, stat],
+        out_specs=here,
+        out_shape=jax.ShapeDtypeStruct(grads.shape, jnp.float32),
         compiler_params=pltpu.CompilerParams(vmem_limit_bytes=48 << 20),
         cost_estimate=pl.CostEstimate(
-            flops=6 * HEAD_DIM * work, bytes_accessed=6 << 20, transcendentals=work
+            flops=16 * HEAD_DIM * work, bytes_accessed=12 << 20, transcendentals=work
         ),
     )(queries, grads, attended, keys, values, own_keys, own_values, *bounds, top, inverse)
 
@@ -313,26 +342,36 @@
         jnp.minimum(position - start, span - 1),
     )
 
-    hidden_grad = narrow_total(hidden_part)
-    gate = narrow_total(gate_part)
-    up = narrow_total(up_part)
-
+    lows = [part.astype(jnp.bfloat16) for part in (hidden_part, gate_part, up_part)]
+    hidden_grad = narrow_total(hidden_part, lows[0])
+    gate = narrow_total(gate_part, lows[1])
+    up = narrow_total(up_part, lows[2])
+
+    queries, own_keys, own_values = after((queries, own_keys, own_values), *lows)
+    early = groups - groups // 4
     outs, tops, totals = [], [], []
-    for group in range(groups):
-        out, top, total = forward_group(
-            group, per_group, base, queries, cache_key, cache_value, own_keys, own_values, bounds
+    for first, count in ((0, early), (early, groups - early)):
+        if count == 0:
+            continue
+        if first:
+            (queries,) = after((queries,), hidden_grad, gate, up)
+        out, top, total = forward(
+            first, count, per_group, base, queries, cache_key, cache_value, own_keys,
+            own_values, bounds,
         )
         outs.append(out)
-        tops.append(top[:, :per_group])
-        totals.append(total[:, :per_group])
+        tops.append(top[:, : count * per_group])
+        totals.append(total[:, : count * per_group])
+    local_out = jnp.concatenate(outs, axis=1)
     local_top = jnp.concatenate(tops, axis=1)
     stats = doubled(
         jnp.concatenate([local_top] + totals, axis=1), functools.partial(merge_softmax, base)
     )
     top, inverse = stats[:, :heads], 1.0 / stats[:, heads:]
     factor = jnp.exp2((local_top - top) * base) * inverse
-    spread = jnp.repeat(factor, HEAD_DIM, axis=1)
-    attended_part = jnp.concatenate(outs, axis=1) * spread
+    owner = jnp.arange(heads * HEAD_DIM, dtype=jnp.int32)[None, :] // HEAD_DIM
+    choose = (owner == jnp.arange(heads, dtype=jnp.int32)[:, None]).astype(jnp.float32)
+    attended_part = local_out * jnp.dot(factor, choose, precision=lax.Precision.HIGHEST)
     side = ((0, 0), (0, HEAD_DIM - heads))
     top, inverse = jnp.pad(top, side), jnp.pad(inverse, side)
     ways = orders()
@@ -346,9 +385,6 @@
 
     activated, d_gate, d_up = swiglu_back(gate, up, hidden_grad)
     d_normed_part = contract_cols(d_gate, w_gate) + contract_cols(d_up, w_up)
-    grad_w_down = contract_rows(activated, grad_out).astype(jnp.bfloat16)
-    grad_w_gate = contract_rows(normed, d_gate).astype(jnp.bfloat16)
-    grad_w_up = contract_rows(normed, d_up).astype(jnp.bfloat16)
     d_normed = jnp.concatenate(
         [
             scatter_sum(as_cube(part), way)
@@ -376,15 +412,13 @@
             grad_residual, (wide_place * columns) % width, columns, 1
         )
         holder = (wide_place * columns) // width == lax.axis_index("narrow")
-        panel = jnp.where(holder, own_panel, swapped(own_panel, "narrow", 0))
+        panel = jnp.where(holder, own_panel, swapped(own_panel, "narrow", 1))
     else:
         whole = lax.all_gather(grad_residual, "narrow", axis=1, tiled=True)
         panel = lax.dynamic_slice_in_dim(whole, wide_place * columns, columns, 1)
-    grad_w_output = contract_rows(attended, panel).astype(jnp.bfloat16)
-
     pieces = 2 if groups % 2 == 0 else 1
     group_count = groups // pieces
-    query_grads = []
+    query_grads, query_parts = [], []
     for piece in range(pieces):
         way = ways[piece]
         wide_rows = group_count * per_group * HEAD_DIM
@@ -392,19 +426,20 @@
         d_attention = gathered(
             scatter_sum(as_cube(contract_cols(panel, rows)), way).astype(jnp.bfloat16), way
         )
-        parts = [
-            backward_group(
-                group, per_group, base, scale, queries, d_attention, attended, cache_key,
-                cache_value, own_keys, own_values, bounds, top, inverse,
-                piece * group_count * per_group,
-            )
-            for group in range(piece * group_count, (piece + 1) * group_count)
-        ]
-        query_part = jnp.concatenate(parts, axis=1)
+        query_part = backward(
+            piece * group_count, group_count, per_group, base, scale, queries, d_attention,
+            attended, cache_key, cache_value, own_keys, own_values, bounds, top, inverse,
+        )
+        query_parts.append(query_part)
         query_grads.append(
             gathered(scatter_sum(as_cube(query_part), way).astype(jnp.bfloat16), way)
         )
     grad_query = jnp.concatenate(query_grads, axis=1)
+    activated, d_gate, d_up, panel = after((activated, d_gate, d_up, panel), *query_parts)
+    grad_w_down = contract_rows(activated, grad_out).astype(jnp.bfloat16)
+    grad_w_gate = contract_rows(normed, d_gate).astype(jnp.bfloat16)
+    grad_w_up = contract_rows(normed, d_up).astype(jnp.bfloat16)
+    grad_w_output = contract_rows(attended, panel).astype(jnp.bfloat16)
     return (
         grad_residual,
         grad_gain,

time: 481 us -> 476 us (0.990); the launches traced: 472 us -> 472 us
  starting transfers between devices: 78.9 us -> 108 us
  local copies, waits for them, and re-layouts: 27.1 us -> 7.78 us
  other arithmetic: 32.1 us -> 25.4 us
  matrix products: 69.3 us -> 63.8 us
  waiting for transfers between devices: 159 us -> 164 us
    ppermute x84 -> x100, starting transfers between devices: 78.9 us -> 108 us  [swapped(): return lax.ppermute(array, axis, [(i, i ^ mask) for i in range(size)])]
    unnamed x74 -> x42, local copies, waits for them, and re-layouts: 9.38 us -> 1.88 us
    dot_general x4, matrix products: 30.2 us -> 24 us  [contract_rows(): lax.dot_general(left, right, (((0,), (0,)), ((), ())), preferred_element_...]
    reshape x1 -> x0, local copies, waits for them, and re-layouts: 5.83 us -> none  [per_device(): spread = jnp.repeat(factor, HEAD_DIM, axis=1)]
    convert_element_type x0 -> x10, other arithmetic: none -> 4.95 us  [the longest x1 1.99 us: swiglu_back(): activated = (silu_gate * up).astype(jnp.bfloat16)]
    ppermute x84 -> x100, waiting for transfers between devices: 159 us -> 164 us  [swapped(): return lax.ppermute(array, axis, [(i, i ^ mask) for i in range(size)])]
    add x28 -> x12, other arithmetic: 6.06 us -> 1.18 us  [the longest x4 0.61 us: doubled(): value = combine(value, swapped(value, 'wide', 1 << k))]
    pallas_call x8 -> x4, Pallas kernels: 102 us -> 100 us  [the longest x2 51.4 us: forward(): pl.pallas_call(functools.partial(forward_kernel, per_group, base), grid=(...]
  transfers between devices with their start and end apart: 84 -> 100, of which waited for: 49 -> 47; matrix products, arithmetic and copies ran while one was open for 24% -> 18% of each run, Pallas kernels for 16% -> 18%
where the time goes in v2:
time: 476 us; the launch traced here: 472 us
  waiting for transfers between devices  164 us (34%)
  starting transfers between devices  108 us (23%)
  Pallas kernels  100 us (21%)
  matrix products  63.8 us (13%)
  other arithmetic  25.4 us (5%)
  local copies, waits for them, and re-layouts  7.78 us (2%)
    ppermute x100, waiting for transfers between devices, swapped(): return lax.ppermute(array, axis, [(i, i ^ mask) for i in range(size)])  164 us
    ppermute x100, starting transfers between devices, swapped(): return lax.ppermute(array, axis, [(i, i ^ mask) for i in range(size)])  108 us
    pallas_call x2, Pallas kernels, forward(): pl.pallas_call(functools.partial(forward_kernel, per_group, base), grid=(...  51.4 us
    pallas_call x2, Pallas kernels, backward(): pl.pallas_call(functools.partial(backward_kernel, first, per_group, base,...  49.1 us
    dot_general x4, matrix products, contract_rows(): lax.dot_general(left, right, (((0,), (0,)), ((), ())), preferred_element_...  24 us
    dot_general x5, matrix products, contract_cols(): lax.dot_general(left, right, (((1,), (1,)), ((), ())), preferred_element_...  22.8 us
  transfers between devices with their start and end apart: 100, of which 47 were waited for; matrix products, arithmetic and copies ran while one was open for 18% of the time, Pallas kernels for 18%

profile of v2, /device:TPU:0, one launch (start us, length us, event | category | flops | bytes accessed | tf_op | source)
XLA Modules:
  0.0 472.0 jit_solution(1016236622940596822)
XLA Ops:
  2.6 3.0 collective-permute-start
  10.7 10.9 %fusion.44 = (bf16[384,1728]{0,1:T(8,128)(2,1)}, f32[384,1728]{0,1:T(8,128)}) fusion(bf16[384,2560]{1,0:T(8,128)(2,1)} %param.15, bf16[1728,2560]{1,0:T(8,128)(2,1)} %param.18), kind=kOutput, calls=%fused_computation.295 | convolution fusion | flops 3398049792 | bytes 14794752 | tf_op jit(solution)/shard_map/dot_general | solution.py:25
  24.4 7.7 %fusion.43 = (bf16[384,1728]{0,1:T(8,128)(2,1)S(1)}, f32[384,1728]{0,1:T(8,128)S(1)}) fusion(bf16[2560,1728]{0,1:T(8,128)(2,1)} %param.16, bf16[384,2560]{1,0:T(8,128)(2,1)S(1)} %copy-done.2, f32[2560]{0:T(1024)S(1)} %convert_element_type.284, f32[384]{0:T(512)S(1)} %add_rsqrt_fusion), kind=kOutput, calls=%fused_computation.294 | convolution fusion | flops 3401981952 | bytes 14806528 | tf_op jit(solution)/shard_map/dot_general | solution.py:325
  32.9 7.4 %fusion.42 = (bf16[384,1728]{0,1:T(8,128)(2,1)S(1)}, f32[384,1728]{0,1:T(8,128)S(1)}) fusion(bf16[2560,1728]{0,1:T(8,128)(2,1)} %param.17, bf16[384,2560]{1,0:T(8,128)(2,1)S(1)} %copy-done.2, f32[2560]{0:T(1024)S(1)} %convert_element_type.284, f32[384]{0:T(512)S(1)} %add_rsqrt_fusion), kind=kOutput, calls=%fused_computation.293 | convolution fusion | flops 3401981952 | bytes 14806528 | tf_op jit(solution)/shard_map/dot_general | solution.py:326
  49.0 38.1 %shard_map.180 = (f32[384,1920]{1,0:T(8,128)S(1)}, f32[384,128]{1,0:T(8,128)S(1)}, f32[384,128]{1,0:T(8,128)S(1)}) custom-call(bf16[384,2560]{1,0:T(8,128)(2,1)S(1)} %pad_maximum_fusion.1.q_ref, bf16[2048,512]{1,0:T(8,128)(2,1)S(1)} %copy-done, bf16[2048,512]{1,0:T(8,128)(2,1)S(1)} %copy-done.1, bf16[128,512]{1,0:T(8,128)(2,1)S(1)} %pad.14.own_key_ref, ...), custom_call_target="tpu_custom_call" | custom-call | flops 25669140480 | bytes 20971520 | tf_op jit(solution)/shard_map/pallas_call | solution.py:255
  87.1 21.6 %collective-permute-done.2 = bf16[384,1728]{0,1:T(8,128)(2,1)S(1)} collective-permute-done((bf16[384,1728]{0,1:T(8,128)(2,1)S(1)}, bf16[384,1728]{0,1:T(8,128)(2,1)S(1)}, u32[]{:S(2)}, u32[]{:S(2)}) %collective-permute-start.2) | collective-permute-done | bytes 1327136 | tf_op jit(solution)/shard_map/ppermute | solution.py:32
  110.7 2.9 multiply_convert_fusion.1
  114.8 13.3 %shard_map.181 = (f32[384,640]{1,0:T(8,128)S(1)}, f32[384,128]{1,0:T(8,128)S(1)}, f32[384,128]{1,0:T(8,128)S(1)}) custom-call(bf16[384,2560]{1,0:T(8,128)(2,1)S(1)} %pad_maximum_fusion.1.q_ref, bf16[2048,512]{1,0:T(8,128)(2,1)S(1)} %copy-done, bf16[2048,512]{1,0:T(8,128)(2,1)S(1)} %copy-done.1, bf16[128,512]{1,0:T(8,128)(2,1)S(1)} %pad.14.own_key_ref, ...), custom_call_target="tpu_custom_call" | custom-call | flops 8556380160 | bytes 20971520 | tf_op jit(solution)/shard_map/pallas_call | solution.py:255
  128.4 3.9 fusion.45
  132.4 6.6 %convolution_add_fusion = f32[384,2560]{1,0:T(8,128)S(1)} fusion(f32[384,2560]{1,0:T(8,128)S(1)} %fusion.45, bf16[384,1728]{0,1:T(8,128)(2,1)S(1)} %get-tuple-element.32, bf16[2560,1728]{0,1:T(8,128)(2,1)} %param.17), kind=kOutput, calls=%fused_computation.6 | convolution fusion | flops 3398369280 | bytes 18038784 | tf_op jit(solution)/shard_map/dot_general | solution.py:25
  141.4 5.2 %collective-permute-done.47 = f32[384,40]{1,0:T(8,128)S(1)} collective-permute-done((f32[384,40]{1,0:T(8,128)S(1)}, f32[384,40]{1,0:T(8,128)S(1)}, u32[]{:S(2)}, u32[]{:S(2)}) %collective-permute-start.47) | collective-permute-done | bytes 61472 | tf_op jit(solution)/shard_map/ppermute | solution.py:32
  148.8 4.7 collective-permute-done.48
  153.8 2.8 collective-permute-start.49
  157.2 7.4 %collective-permute-done.49 = f32[384,40]{1,0:T(8,128)S(1)} collective-permute-done((f32[384,40]{1,0:T(8,128)S(1)}, f32[384,40]{1,0:T(8,128)S(1)}, u32[]{:S(2)}, u32[]{:S(2)}) %collective-permute-start.49) | collective-permute-done | bytes 61472 | tf_op jit(solution)/shard_map/ppermute | solution.py:32
  168.7 2.9 collective-permute-start.12
  173.2 5.1 %collective-permute-done.12 = bf16[1,2,1,1,24,1280]{5,4,3,2,1,0:T(8,128)(2,1)S(1)} collective-permute-done((bf16[1,2,1,1,24,1280]{5,4,3,2,1,0:T(8,128)(2,1)S(1)}, bf16[1,2,1,1,24,1280]{5,4,3,2,1,0:T(8,128)(2,1)S(1)}, u32[]{:S(2)}, u32[]{:S(2)}) %collective-permute-start.12) | collective-permute-done | bytes 122912 | tf_op jit(solution)/shard_map/ppermute | solution.py:32
  178.4 4.8 %collective-permute-done.11 = bf16[1,2,1,1,24,1280]{5,4,3,2,1,0:T(8,128)(2,1)S(1)} collective-permute-done((bf16[1,2,1,1,24,1280]{5,4,3,2,1,0:T(8,128)(2,1)S(1)}, bf16[1,2,1,1,24,1280]{5,4,3,2,1,0:T(8,128)(2,1)S(1)}, u32[]{:S(2)}, u32[]{:S(2)}) %collective-permute-start.11) | collective-permute-done | bytes 122912 | tf_op jit(solution)/shard_map/ppermute | solution.py:32
  185.5 2.8 collective-permute-done.13
  190.1 3.8 collective-permute-done.5
  194.1 2.7 collective-permute-start.8
  211.3 2.5 collective-permute-done.26
  218.8 4.5 collective-permute-done.28
  225.8 2.5 collective-permute-start.15
  229.6 2.9 collective-permute-done.20
  236.0 2.6 collective-permute-start.21
  241.0 4.6 collective-permute-done.65
  252.0 6.7 %collective-permute-done.53 = bf16[1,1,1,1,24,1280]{5,4,3,2,1,0:T(8,128)(2,1)S(1)} collective-permute-done((bf16[1,1,1,1,24,1280]{5,4,3,2,1,0:T(8,128)(2,1)S(1)}, bf16[1,1,1,1,24,1280]{5,4,3,2,1,0:T(8,128)(2,1)S(1)}, u32[]{:S(2)}, u32[]{:S(2)}) %collective-permute-start.53) | collective-permute-done | bytes 61472 | tf_op jit(solution)/shard_map/ppermute | solution.py:32
  258.9 2.4 collective-permute-start.56
  261.3 3.1 collective-permute-done.55
  266.3 4.2 collective-permute-done.57
  273.1 5.9 %collective-permute-done.58 = bf16[1,1,2,2,24,1280]{5,4,3,2,1,0:T(8,128)(2,1)S(1)} collective-permute-done((bf16[1,1,2,2,24,1280]{5,4,3,2,1,0:T(8,128)(2,1)S(1)}, bf16[1,1,2,2,24,1280]{5,4,3,2,1,0:T(8,128)(2,1)S(1)}, u32[]{:S(2)}, u32[]{:S(2)}) %collective-permute-start.58) | collective-permute-done | bytes 245792 | tf_op jit(solution)/shard_map/ppermute | solution.py:32
  284.5 5.1 %collective-permute-done.29 = bf16[384,320]{1,0:T(8,128)(2,1)S(1)} collective-permute-done((bf16[384,320]{1,0:T(8,128)(2,1)S(1)}, bf16[384,320]{1,0:T(8,128)(2,1)S(1)}, u32[]{:S(2)}, u32[]{:S(2)}) %collective-permute-start.29) | collective-permute-done | bytes 245792 | tf_op jit(solution)/shard_map/ppermute | solution.py:32
  298.3 2.8 collective-permute-done.73
  301.1 5.8 %collective-permute-done.72 = bf16[1,2,1,1,24,1280]{5,4,3,2,1,0:T(8,128)(2,1)S(1)} collective-permute-done((bf16[1,2,1,1,24,1280]{5,4,3,2,1,0:T(8,128)(2,1)S(1)}, bf16[1,2,1,1,24,1280]{5,4,3,2,1,0:T(8,128)(2,1)S(1)}, u32[]{:S(2)}, u32[]{:S(2)}) %collective-permute-start.72) | collective-permute-done | bytes 122912 | tf_op jit(solution)/shard_map/ppermute | solution.py:32
  309.2 2.8 collective-permute-done.74
  312.4 3.5 collective-permute-done.37
  331.7 7.5 %collective-permute-done.42 = bf16[1,1,1,1,24,1280]{5,4,3,2,1,0:T(8,128)(2,1)S(1)} collective-permute-done((bf16[1,1,1,1,24,1280]{5,4,3,2,1,0:T(8,128)(2,1)S(1)}, bf16[1,1,1,1,24,1280]{5,4,3,2,1,0:T(8,128)(2,1)S(1)}, u32[]{:S(2)}, u32[]{:S(2)}) %collective-permute-start.42) | collective-permute-done | bytes 61472 | tf_op jit(solution)/shard_map/ppermute | solution.py:32
  341.1 4.4 collective-permute-done.44
  345.9 24.6 %shard_map.183 = f32[384,1280]{1,0:T(8,128)S(1)} custom-call(bf16[384,2560]{1,0:T(8,128)(2,1)S(1)} %pad_maximum_fusion.1.q_ref, bf16[384,1280]{1,0:T(8,128)(2,1)S(1)} %bitcast.62, bf16[384,2560]{1,0:T(8,128)(2,1)} %pad_maximum_fusion.2.attended_ref, bf16[2048,512]{1,0:T(8,128)(2,1)} %key_ref.7, bf16[2048,512]{1,0:T(8,128)(2,1)} %value_ref.7, ...), custom_call_target="tpu_custom_call" | custom-call | flops 17112760320 | bytes 12582912 | tf_op jit(solution)/shard_map/pallas_call | solution.py:280
  371.9 24.5 %shard_map.182 = f32[384,1280]{1,0:T(8,128)S(1)} custom-call(bf16[384,2560]{1,0:T(8,128)(2,1)S(1)} %pad_maximum_fusion.1.q_ref, bf16[384,1280]{1,0:T(8,128)(2,1)S(1)} %bitcast.61, bf16[384,2560]{1,0:T(8,128)(2,1)} %pad_maximum_fusion.2.attended_ref, bf16[2048,512]{1,0:T(8,128)(2,1)} %key_ref.7, bf16[2048,512]{1,0:T(8,128)(2,1)} %value_ref.7, ...), custom_call_target="tpu_custom_call" | custom-call | flops 17112760320 | bytes 12582912 | tf_op jit(solution)/shard_map/pallas_call | solution.py:280
  396.6 7.3 %convolution_convert_fusion.1 = bf16[2560,1728]{0,1:T(8,128)(2,1)} fusion(bf16[384,1728]{0,1:T(8,128)(2,1)S(1)} %multiply_convert_fusion.2, bf16[384,2560]{1,0:T(8,128)(2,1)S(1)} %copy-done.3, f32[2560]{0:T(1024)S(1)} %copy-done.10, f32[384]{0:T(512)S(1)} %copy-done.15), kind=kOutput, calls=%fused_computation.1 | convolution fusion | flops 3405742080 | bytes 12152320 | tf_op jit(solution)/shard_map/dot_general | solution.py:19
  403.9 7.5 %convolution_convert_fusion = bf16[2560,1728]{0,1:T(8,128)(2,1)} fusion(bf16[384,1728]{0,1:T(8,128)(2,1)S(1)} %get-tuple-element.32, bf16[384,2560]{1,0:T(8,128)(2,1)S(1)} %copy-done.3, f32[2560]{0:T(1024)S(1)} %copy-done.10, f32[384]{0:T(512)S(1)} %copy-done.15), kind=kOutput, calls=%fused_computation | convolution fusion | flops 3405742080 | bytes 12152320 | tf_op jit(solution)/shard_map/dot_general | solution.py:19
  416.4 7.0 %convolution_convert_fusion.2 = bf16[1728,2560]{1,0:T(8,128)(2,1)} fusion(bf16[384,1728]{0,1:T(8,128)(2,1)S(1)} %copy-done.5, bf16[384,2560]{1,0:T(8,128)(2,1)S(1)} %copy-done.12), kind=kOutput, calls=%fused_computation.2 | convolution fusion | flops 3401809920 | bytes 12140544 | tf_op jit(solution)/shard_map/dot_general | solution.py:19
  423.4 4.2 collective-permute-done.92
  434.3 2.6 collective-permute-done.95
  445.3 3.6 collective-permute-start.83
  459.1 2.7 collective-permute-done.87
  463.3 4.9 %collective-permute-done.88 = bf16[1,1,2,2,24,1280]{5,4,3,2,1,0:T(8,128)(2,1)S(1)} collective-permute-done((bf16[1,1,2,2,24,1280]{5,4,3,2,1,0:T(8,128)(2,1)S(1)}, bf16[1,1,2,2,24,1280]{5,4,3,2,1,0:T(8,128)(2,1)S(1)}, u32[]{:S(2)}, u32[]{:S(2)}) %collective-permute-start.88) | collective-permute-done | bytes 245792 | tf_op jit(solution)/shard_map/ppermute | solution.py:32
  (370 shorter events, 149.1 us)
Async XLA Ops:
  2.6 21.7 %collective-permute-start = (f32[384]{0:T(512)S(1)}, f32[384]{0:T(512)S(1)}, u32[]{:S(2)}, u32[]{:S(2)}) collective-permute-start(f32[384]{0:T(512)S(1)} %fusion), channel_id=1, source_target_pairs={{0,1},{1,0},{2,3},{3,2},{4,5},{5,4},{6,7},{7,6},{8,9},{9,8},{10,11... | collective-permute-start | bytes 4616 | tf_op jit(solution)/shard_map/ppermute | solution.py:32
  6.5 26.3 %collective-permute-start.34 = (bf16[96,512]{1,0:T(8,128)(2,1)S(1)}, bf16[96,512]{1,0:T(8,128)(2,1)}, u32[]{:S(2)}, u32[]{:S(2)}) collective-permute-start(bf16[96,512]{1,0:T(8,128)(2,1)S(1)} %dynamic_slice.315), channel_id=1, source_target_pairs={{0,1},{1,0},{2,3},{3,2},{4,5},{5,4},{6,7},{7,6},{8,9},{9,8},{10,11... | collective-permute-start | bytes 294920 | tf_op jit(solution)/shard_map/ppermute | solution.py:32
  7.5 32.9 %collective-permute-start.32 = (bf16[96,512]{1,0:T(8,128)(2,1)S(1)}, bf16[96,512]{1,0:T(8,128)(2,1)}, u32[]{:S(2)}, u32[]{:S(2)}) collective-permute-start(bf16[96,512]{1,0:T(8,128)(2,1)S(1)} %dynamic_slice.312), channel_id=1, source_target_pairs={{0,1},{1,0},{2,3},{3,2},{4,5},{5,4},{6,7},{7,6},{8,9},{9,8},{10,11... | collective-permute-start | bytes 294920 | tf_op jit(solution)/shard_map/ppermute | solution.py:32
  10.6 32.8 %collective-permute-start.30 = (bf16[96,2560]{1,0:T(8,128)(2,1)S(1)}, bf16[96,2560]{1,0:T(8,128)(2,1)}, u32[]{:S(2)}, u32[]{:S(2)}) collective-permute-start(bf16[96,2560]{1,0:T(8,128)(2,1)S(1)} %dynamic_slice.310), channel_id=1, source_target_pairs={{0,1},{1,0},{2,3},{3,2},{4,5},{5,4},{6,7},{7,6},{8,9},{9,8},{10,11... | collective-permute-start | bytes 1474568 | tf_op jit(solution)/shard_map/ppermute | solution.py:32
  21.6 89.1 %collective-permute-start.1 = (bf16[384,1728]{0,1:T(8,128)(2,1)}, bf16[384,1728]{0,1:T(8,128)(2,1)}, u32[]{:S(2)}, u32[]{:S(2)}) collective-permute-start(bf16[384,1728]{0,1:T(8,128)(2,1)} %get-tuple-element.194), channel_id=1, source_target_pairs={{0,1},{1,0},{2,3},{3,2},{4,5},{5,4},{6,7},{7,6},{8,9},{9,8},{10,11... | collective-permute-start | bytes 3981320 | tf_op jit(solution)/shard_map/ppermute | solution.py:32
  32.7 54.4 %collective-permute-start.3 = (bf16[384,1728]{0,1:T(8,128)(2,1)S(1)}, bf16[384,1728]{0,1:T(8,128)(2,1)S(1)}, u32[]{:S(2)}, u32[]{:S(2)}) collective-permute-start(bf16[384,1728]{0,1:T(8,128)(2,1)S(1)} %get-tuple-element.192), channel_id=1, source_target_pairs={{0,1},{1,0},{2,3},{3,2},{4,5},{5,4},{6,7},{7,6},{8,9},{9,8},{10,11... | collective-permute-start | bytes 3981320 | tf_op jit(solution)/shard_map/ppermute | solution.py:32
  32.9 9.4 %collective-permute-start.35 = (bf16[96,512]{1,0:T(8,128)(2,1)}, bf16[96,512]{1,0:T(8,128)(2,1)S(1)}, u32[]{:S(2)}, u32[]{:S(2)}) collective-permute-start(bf16[96,512]{1,0:T(8,128)(2,1)} %collective-permute-done.34), channel_id=1, source_target_pairs={{0,2},{2,0},{4,6},{6,4},{8,10},{10,8},{12,14},{14,12},{16,18},{18,... | collective-permute-start | bytes 294920 | tf_op jit(solution)/shard_map/ppermute | solution.py:32
  40.3 68.4 %collective-permute-start.2 = (bf16[384,1728]{0,1:T(8,128)(2,1)S(1)}, bf16[384,1728]{0,1:T(8,128)(2,1)S(1)}, u32[]{:S(2)}, u32[]{:S(2)}) collective-permute-start(bf16[384,1728]{0,1:T(8,128)(2,1)S(1)} %get-tuple-element.190), channel_id=1, source_target_pairs={{0,1},{1,0},{2,3},{3,2},{4,5},{5,4},{6,7},{7,6},{8,9},{9,8},{10,11... | collective-permute-start | bytes 3981320 | tf_op jit(solution)/shard_map/ppermute | solution.py:32
  128.3 10.6 %collective-permute-start.46 = (f32[384,40]{1,0:T(8,128)S(1)}, f32[384,40]{1,0:T(8,128)S(1)}, u32[]{:S(2)}, u32[]{:S(2)}) collective-permute-start(f32[384,40]{1,0:T(8,128)S(1)} %pad_maximum_fusion.37), channel_id=1, source_target_pairs={{0,2},{2,0},{4,6},{6,4},{8,10},{10,8},{12,14},{14,12},{16,18},{18,... | collective-permute-start | bytes 184328 | tf_op jit(solution)/shard_map/ppermute | solution.py:32
  153.8 10.9 %collective-permute-start.49 = (f32[384,40]{1,0:T(8,128)S(1)}, f32[384,40]{1,0:T(8,128)S(1)}, u32[]{:S(2)}, u32[]{:S(2)}) collective-permute-start(f32[384,40]{1,0:T(8,128)S(1)} %pad_maximum_fusion.40), channel_id=1, source_target_pairs={{0,16},{2,18},{4,20},{6,22},{8,24},{10,26},{12,28},{14,30},{16,0},... | collective-permute-start | bytes 184328 | tf_op jit(solution)/shard_map/ppermute | solution.py:32
  156.6 15.0 %collective-permute-start.4 = (bf16[1,2,2,2,24,1280]{5,4,3,2,1,0:T(8,128)(2,1)S(1)}, bf16[1,2,2,2,24,1280]{5,4,3,2,1,0:T(8,128)(2,1)S(1)}, u32[]{:S(2)}, u32[]{:S(2)}) collective-permute-start(bf16[1,2,2,2,24,1280]{5,4,3,2,1,0:T(8,128)(2,1)S(1)} %dynamic-slice_convert_fusion.7), channel_id=1, source_target_pairs={{0,2},{2,0},{4,6},{6,4},{8,10},{10,8},{12,14},{14,12},{16,18},{18,... | collective-permute-start | bytes 1474568 | tf_op jit(solution)/shard_map/ppermute | solution.py:32
  156.7 11.0 %collective-permute-start.9 = (bf16[1,2,2,2,24,1280]{5,4,3,2,1,0:T(8,128)(2,1)S(1)}, bf16[1,2,2,2,24,1280]{5,4,3,2,1,0:T(8,128)(2,1)S(1)}, u32[]{:S(2)}, u32[]{:S(2)}) collective-permute-start(bf16[1,2,2,2,24,1280]{5,4,3,2,1,0:T(8,128)(2,1)S(1)} %dynamic-slice_convert_fusion.6), channel_id=1, source_target_pairs={{0,2},{2,0},{4,6},{6,4},{8,10},{10,8},{12,14},{14,12},{16,18},{18,... | collective-permute-start | bytes 1474568 | tf_op jit(solution)/shard_map/ppermute | solution.py:32
  167.1 21.2 %collective-permute-start.50 = (bf16[1,2,2,2,24,1280]{5,4,3,2,1,0:T(8,128)(2,1)S(1)}, bf16[1,2,2,2,24,1280]{5,4,3,2,1,0:T(8,128)(2,1)S(1)}, u32[]{:S(2)}, u32[]{:S(2)}) collective-permute-start(bf16[1,2,2,2,24,1280]{5,4,3,2,1,0:T(8,128)(2,1)S(1)} %dynamic-slice_convert_fusion.4), channel_id=1, source_target_pairs={{0,2},{2,0},{4,6},{6,4},{8,10},{10,8},{12,14},{14,12},{16,18},{18,... | collective-permute-start | bytes 1474568 | tf_op jit(solution)/shard_map/ppermute | solution.py:32
  167.2 30.3 %collective-permute-start.60 = (bf16[1,2,2,2,24,1280]{5,4,3,2,1,0:T(8,128)(2,1)S(1)}, bf16[1,2,2,2,24,1280]{5,4,3,2,1,0:T(8,128)(2,1)S(1)}, u32[]{:S(2)}, u32[]{:S(2)}) collective-permute-start(bf16[1,2,2,2,24,1280]{5,4,3,2,1,0:T(8,128)(2,1)S(1)} %dynamic-slice_convert_fusion.3), channel_id=1, source_target_pairs={{0,2},{2,0},{4,6},{6,4},{8,10},{10,8},{12,14},{14,12},{16,18},{18,... | collective-permute-start | bytes 1474568 | tf_op jit(solution)/shard_map/ppermute | solution.py:32
  168.7 9.7 %collective-permute-start.12 = (bf16[1,2,1,1,24,1280]{5,4,3,2,1,0:T(8,128)(2,1)S(1)}, bf16[1,2,1,1,24,1280]{5,4,3,2,1,0:T(8,128)(2,1)S(1)}, u32[]{:S(2)}, u32[]{:S(2)}) collective-permute-start(bf16[1,2,1,1,24,1280]{5,4,3,2,1,0:T(8,128)(2,1)S(1)} %get-tuple-element.120), channel_id=1, source_target_pairs={{0,24},{2,26},{4,28},{6,30},{8,16},{10,18},{12,20},{14,22},{16,8},... | collective-permute-start | bytes 368648 | tf_op jit(solution)/shard_map/ppermute | solution.py:32
  171.6 11.6 %collective-permute-start.11 = (bf16[1,2,1,1,24,1280]{5,4,3,2,1,0:T(8,128)(2,1)S(1)}, bf16[1,2,1,1,24,1280]{5,4,3,2,1,0:T(8,128)(2,1)S(1)}, u32[]{:S(2)}, u32[]{:S(2)}) collective-permute-start(bf16[1,2,1,1,24,1280]{5,4,3,2,1,0:T(8,128)(2,1)S(1)} %get-tuple-element.121), channel_id=1, source_target_pairs={{0,16},{2,18},{4,20},{6,22},{8,24},{10,26},{12,28},{14,30},{16,0},... | collective-permute-start | bytes 368648 | tf_op jit(solution)/shard_map/ppermute | solution.py:32
  184.9 9.0 %collective-permute-start.5 = (bf16[1,1,2,2,24,1280]{5,4,3,2,1,0:T(8,128)(2,1)S(1)}, bf16[1,1,2,2,24,1280]{5,4,3,2,1,0:T(8,128)(2,1)S(1)}, u32[]{:S(2)}, u32[]{:S(2)}) collective-permute-start(bf16[1,1,2,2,24,1280]{5,4,3,2,1,0:T(8,128)(2,1)S(1)} %dynamic-slice_convert_fusion.11), channel_id=1, source_target_pairs={{0,4},{2,6},{4,0},{6,2},{8,12},{10,14},{12,8},{14,10},{16,20},{18,... | collective-permute-start | bytes 737288 | tf_op jit(solution)/shard_map/ppermute | solution.py:32
  188.5 50.8 %collective-permute-start.51 = (bf16[1,1,2,2,24,1280]{5,4,3,2,1,0:T(8,128)(2,1)S(1)}, bf16[1,1,2,2,24,1280]{5,4,3,2,1,0:T(8,128)(2,1)S(1)}, u32[]{:S(2)}, u32[]{:S(2)}) collective-permute-start(bf16[1,1,2,2,24,1280]{5,4,3,2,1,0:T(8,128)(2,1)S(1)} %dynamic-slice_convert_fusion.9), channel_id=1, source_target_pairs={{0,4},{2,6},{4,0},{6,2},{8,12},{10,14},{12,8},{14,10},{16,20},{18,... | collective-permute-start | bytes 737288 | tf_op jit(solution)/shard_map/ppermute | solution.py:32
  203.0 22.7 %collective-permute-start.61 = (bf16[1,2,1,1,24,1280]{5,4,3,2,1,0:T(8,128)(2,1)S(1)}, bf16[1,2,1,1,24,1280]{5,4,3,2,1,0:T(8,128)(2,1)S(1)}, u32[]{:S(2)}, u32[]{:S(2)}) collective-permute-start(bf16[1,2,1,1,24,1280]{5,4,3,2,1,0:T(8,128)(2,1)S(1)} %get-tuple-element.110), channel_id=1, source_target_pairs={{0,8},{2,10},{4,12},{6,14},{8,0},{10,2},{12,4},{14,6},{16,24},{18,... | collective-permute-start | bytes 368648 | tf_op jit(solution)/shard_map/ppermute | solution.py:32
  203.6 22.2 %collective-permute-start.63 = (bf16[1,2,1,1,24,1280]{5,4,3,2,1,0:T(8,128)(2,1)S(1)}, bf16[1,2,1,1,24,1280]{5,4,3,2,1,0:T(8,128)(2,1)S(1)}, u32[]{:S(2)}, u32[]{:S(2)}) collective-permute-start(bf16[1,2,1,1,24,1280]{5,4,3,2,1,0:T(8,128)(2,1)S(1)} %get-tuple-element.111), channel_id=1, source_target_pairs={{0,24},{2,26},{4,28},{6,30},{8,16},{10,18},{12,20},{14,22},{16,8},... | collective-permute-start | bytes 368648 | tf_op jit(solution)/shard_map/ppermute | solution.py:32
  205.0 23.4 %collective-permute-start.62 = (bf16[1,2,1,1,24,1280]{5,4,3,2,1,0:T(8,128)(2,1)S(1)}, bf16[1,2,1,1,24,1280]{5,4,3,2,1,0:T(8,128)(2,1)S(1)}, u32[]{:S(2)}, u32[]{:S(2)}) collective-permute-start(bf16[1,2,1,1,24,1280]{5,4,3,2,1,0:T(8,128)(2,1)S(1)} %get-tuple-element.112), channel_id=1, source_target_pairs={{0,16},{2,18},{4,20},{6,22},{8,24},{10,26},{12,28},{14,30},{16,0},... | collective-permute-start | bytes 368648 | tf_op jit(solution)/shard_map/ppermute | solution.py:32
  223.3 12.7 %collective-permute-start.17 = (bf16[1,1,1,1,24,1280]{5,4,3,2,1,0:T(8,128)(2,1)S(1)}, bf16[1,1,1,1,24,1280]{5,4,3,2,1,0:T(8,128)(2,1)S(1)}, u32[]{:S(2)}, u32[]{:S(2)}) collective-permute-start(bf16[1,1,1,1,24,1280]{5,4,3,2,1,0:T(8,128)(2,1)S(1)} %get-tuple-element.188), channel_id=1, source_target_pairs={{0,24},{2,26},{4,28},{6,30},{8,16},{10,18},{12,20},{14,22},{16,8},... | collective-permute-start | bytes 184328 | tf_op jit(solution)/shard_map/ppermute | solution.py:32
  225.7 10.3 %collective-permute-start.16 = (bf16[1,1,1,1,24,1280]{5,4,3,2,1,0:T(8,128)(2,1)S(1)}, bf16[1,1,1,1,24,1280]{5,4,3,2,1,0:T(8,128)(2,1)S(1)}, u32[]{:S(2)}, u32[]{:S(2)}) collective-permute-start(bf16[1,1,1,1,24,1280]{5,4,3,2,1,0:T(8,128)(2,1)S(1)} %get-tuple-element.188), channel_id=1, source_target_pairs={{0,16},{2,18},{4,20},{6,22},{8,24},{10,26},{12,28},{14,30},{16,0},... | collective-permute-start | bytes 184328 | tf_op jit(solution)/shard_map/ppermute | solution.py:32
  234.2 13.4 %collective-permute-start.23 = (bf16[1,2,1,1,24,1280]{5,4,3,2,1,0:T(8,128)(2,1)S(1)}, bf16[1,2,1,1,24,1280]{5,4,3,2,1,0:T(8,128)(2,1)S(1)}, u32[]{:S(2)}, u32[]{:S(2)}) collective-permute-start(bf16[1,2,1,1,24,1280]{5,4,3,2,1,0:T(8,128)(2,1)S(1)} %pad_maximum_fusion.43), channel_id=1, source_target_pairs={{0,24},{2,26},{4,28},{6,30},{8,16},{10,18},{12,20},{14,22},{16,8},... | collective-permute-start | bytes 368648 | tf_op jit(solution)/shard_map/ppermute | solution.py:32
  236.0 13.3 %collective-permute-start.22 = (bf16[1,2,1,1,24,1280]{5,4,3,2,1,0:T(8,128)(2,1)S(1)}, bf16[1,2,1,1,24,1280]{5,4,3,2,1,0:T(8,128)(2,1)S(1)}, u32[]{:S(2)}, u32[]{:S(2)}) collective-permute-start(bf16[1,2,1,1,24,1280]{5,4,3,2,1,0:T(8,128)(2,1)S(1)} %pad_maximum_fusion.43), channel_id=1, source_target_pairs={{0,16},{2,18},{4,20},{6,22},{8,24},{10,26},{12,28},{14,30},{16,0},... | collective-permute-start | bytes 368648 | tf_op jit(solution)/shard_map/ppermute | solution.py:32
  236.0 9.6 %collective-permute-start.21 = (bf16[1,2,1,1,24,1280]{5,4,3,2,1,0:T(8,128)(2,1)S(1)}, bf16[1,2,1,1,24,1280]{5,4,3,2,1,0:T(8,128)(2,1)S(1)}, u32[]{:S(2)}, u32[]{:S(2)}) collective-permute-start(bf16[1,2,1,1,24,1280]{5,4,3,2,1,0:T(8,128)(2,1)S(1)} %pad_maximum_fusion.43), channel_id=1, source_target_pairs={{0,8},{2,10},{4,12},{6,14},{8,0},{10,2},{12,4},{14,6},{16,24},{18,... | collective-permute-start | bytes 368648 | tf_op jit(solution)/shard_map/ppermute | solution.py:32
  238.7 33.7 %collective-permute-start.18 = (bf16[1,1,2,2,24,1280]{5,4,3,2,1,0:T(8,128)(2,1)S(1)}, bf16[1,1,2,2,24,1280]{5,4,3,2,1,0:T(8,128)(2,1)S(1)}, u32[]{:S(2)}, u32[]{:S(2)}) collective-permute-start(bf16[1,1,2,2,24,1280]{5,4,3,2,1,0:T(8,128)(2,1)S(1)} %pad_maximum_fusion.22), channel_id=1, source_target_pairs={{0,4},{2,6},{4,0},{6,2},{8,12},{10,14},{12,8},{14,10},{16,20},{18,... | collective-permute-start | bytes 737288 | tf_op jit(solution)/shard_map/ppermute | solution.py:32
  247.6 11.2 %collective-permute-start.53 = (bf16[1,1,1,1,24,1280]{5,4,3,2,1,0:T(8,128)(2,1)S(1)}, bf16[1,1,1,1,24,1280]{5,4,3,2,1,0:T(8,128)(2,1)S(1)}, u32[]{:S(2)}, u32[]{:S(2)}) collective-permute-start(bf16[1,1,1,1,24,1280]{5,4,3,2,1,0:T(8,128)(2,1)S(1)} %get-tuple-element.139), channel_id=1, source_target_pairs={{0,16},{2,18},{4,20},{6,22},{8,24},{10,26},{12,28},{14,30},{16,0},... | collective-permute-start | bytes 184328 | tf_op jit(solution)/shard_map/ppermute | solution.py:32
  249.3 22.9 %collective-permute-start.68 = (bf16[1,2,1,1,24,1280]{5,4,3,2,1,0:T(8,128)(2,1)S(1)}, bf16[1,2,1,1,24,1280]{5,4,3,2,1,0:T(8,128)(2,1)S(1)}, u32[]{:S(2)}, u32[]{:S(2)}) collective-permute-start(bf16[1,2,1,1,24,1280]{5,4,3,2,1,0:T(8,128)(2,1)S(1)} %pad_maximum_fusion.48), channel_id=1, source_target_pairs={{0,24},{2,26},{4,28},{6,30},{8,16},{10,18},{12,20},{14,22},{16,8},... | collective-permute-start | bytes 368648 | tf_op jit(solution)/shard_map/ppermute | solution.py:32
  251.2 21.0 %collective-permute-start.67 = (bf16[1,2,1,1,24,1280]{5,4,3,2,1,0:T(8,128)(2,1)S(1)}, bf16[1,2,1,1,24,1280]{5,4,3,2,1,0:T(8,128)(2,1)S(1)}, u32[]{:S(2)}, u32[]{:S(2)}) collective-permute-start(bf16[1,2,1,1,24,1280]{5,4,3,2,1,0:T(8,128)(2,1)S(1)} %pad_maximum_fusion.48), channel_id=1, source_target_pairs={{0,16},{2,18},{4,20},{6,22},{8,24},{10,26},{12,28},{14,30},{16,0},... | collective-permute-start | bytes 368648 | tf_op jit(solution)/shard_map/ppermute | solution.py:32
  270.5 8.9 %collective-permute-start.24 = (bf16[1,2,2,2,24,1280]{5,4,3,2,1,0:T(8,128)(2,1)S(1)}, bf16[1,2,2,2,24,1280]{5,4,3,2,1,0:T(8,128)(2,1)S(1)}, u32[]{:S(2)}, u32[]{:S(2)}) collective-permute-start(bf16[1,2,2,2,24,1280]{5,4,3,2,1,0:T(8,128)(2,1)S(1)} %pad_maximum_fusion.14), channel_id=1, source_target_pairs={{0,2},{2,0},{4,6},{6,4},{8,10},{10,8},{12,14},{14,12},{16,18},{18,... | collective-permute-start | bytes 1474568 | tf_op jit(solution)/shard_map/ppermute | solution.py:32
  280.1 9.5 %collective-permute-start.29 = (bf16[384,320]{1,0:T(8,128)(2,1)S(1)}, bf16[384,320]{1,0:T(8,128)(2,1)S(1)}, u32[]{:S(2)}, u32[]{:S(2)}) collective-permute-start(bf16[384,320]{1,0:T(8,128)(2,1)S(1)} %fusion.8), channel_id=1, source_target_pairs={{0,1},{1,0},{2,3},{3,2},{4,5},{5,4},{6,7},{7,6},{8,9},{9,8},{10,11... | collective-permute-start | bytes 737288 | tf_op jit(solution)/shard_map/ppermute | solution.py:32
  294.3 12.6 %collective-permute-start.72 = (bf16[1,2,1,1,24,1280]{5,4,3,2,1,0:T(8,128)(2,1)S(1)}, bf16[1,2,1,1,24,1280]{5,4,3,2,1,0:T(8,128)(2,1)S(1)}, u32[]{:S(2)}, u32[]{:S(2)}) collective-permute-start(bf16[1,2,1,1,24,1280]{5,4,3,2,1,0:T(8,128)(2,1)S(1)} %get-tuple-element.105), channel_id=1, source_target_pairs={{0,16},{2,18},{4,20},{6,22},{8,24},{10,26},{12,28},{14,30},{16,0},... | collective-permute-start | bytes 368648 | tf_op jit(solution)/shard_map/ppermute | solution.py:32
  324.8 16.0 %collective-permute-start.78 = (bf16[1,2,1,1,24,1280]{5,4,3,2,1,0:T(8,128)(2,1)S(1)}, bf16[1,2,1,1,24,1280]{5,4,3,2,1,0:T(8,128)(2,1)S(1)}, u32[]{:S(2)}, u32[]{:S(2)}) collective-permute-start(bf16[1,2,1,1,24,1280]{5,4,3,2,1,0:T(8,128)(2,1)S(1)} %pad_maximum_fusion.49), channel_id=1, source_target_pairs={{0,24},{2,26},{4,28},{6,30},{8,16},{10,18},{12,20},{14,22},{16,8},... | collective-permute-start | bytes 368648 | tf_op jit(solution)/shard_map/ppermute | solution.py:32
  326.7 14.1 %collective-permute-start.77 = (bf16[1,2,1,1,24,1280]{5,4,3,2,1,0:T(8,128)(2,1)S(1)}, bf16[1,2,1,1,24,1280]{5,4,3,2,1,0:T(8,128)(2,1)S(1)}, u32[]{:S(2)}, u32[]{:S(2)}) collective-permute-start(bf16[1,2,1,1,24,1280]{5,4,3,2,1,0:T(8,128)(2,1)S(1)} %pad_maximum_fusion.49), channel_id=1, source_target_pairs={{0,16},{2,18},{4,20},{6,22},{8,24},{10,26},{12,28},{14,30},{16,0},... | collective-permute-start | bytes 368648 | tf_op jit(solution)/shard_map/ppermute | solution.py:32
  327.1 13.7 %collective-permute-start.76 = (bf16[1,2,1,1,24,1280]{5,4,3,2,1,0:T(8,128)(2,1)S(1)}, bf16[1,2,1,1,24,1280]{5,4,3,2,1,0:T(8,128)(2,1)S(1)}, u32[]{:S(2)}, u32[]{:S(2)}) collective-permute-start(bf16[1,2,1,1,24,1280]{5,4,3,2,1,0:T(8,128)(2,1)S(1)} %pad_maximum_fusion.49), channel_id=1, source_target_pairs={{0,8},{2,10},{4,12},{6,14},{8,0},{10,2},{12,4},{14,6},{16,24},{18,... | collective-permute-start | bytes 368648 | tf_op jit(solution)/shard_map/ppermute | solution.py:32
  329.3 9.9 %collective-permute-start.42 = (bf16[1,1,1,1,24,1280]{5,4,3,2,1,0:T(8,128)(2,1)S(1)}, bf16[1,1,1,1,24,1280]{5,4,3,2,1,0:T(8,128)(2,1)S(1)}, u32[]{:S(2)}, u32[]{:S(2)}) collective-permute-start(bf16[1,1,1,1,24,1280]{5,4,3,2,1,0:T(8,128)(2,1)S(1)} %add_convert_fusion.6), channel_id=1, source_target_pairs={{0,16},{2,18},{4,20},{6,22},{8,24},{10,26},{12,28},{14,30},{16,0},... | collective-permute-start | bytes 184328 | tf_op jit(solution)/shard_map/ppermute | solution.py:32
  329.7 9.5 %collective-permute-start.43 = (bf16[1,1,1,1,24,1280]{5,4,3,2,1,0:T(8,128)(2,1)S(1)}, bf16[1,1,1,1,24,1280]{5,4,3,2,1,0:T(8,128)(2,1)S(1)}, u32[]{:S(2)}, u32[]{:S(2)}) collective-permute-start(bf16[1,1,1,1,24,1280]{5,4,3,2,1,0:T(8,128)(2,1)S(1)} %add_convert_fusion.6), channel_id=1, source_target_pairs={{0,24},{2,26},{4,28},{6,30},{8,16},{10,18},{12,20},{14,22},{16,8},... | collective-permute-start | bytes 184328 | tf_op jit(solution)/shard_map/ppermute | solution.py:32
  345.6 26.2 %collective-permute-start.45 = (bf16[1,2,2,2,24,1280]{5,4,3,2,1,0:T(8,128)(2,1)S(1)}, bf16[1,2,2,2,24,1280]{5,4,3,2,1,0:T(8,128)(2,1)S(1)}, u32[]{:S(2)}, u32[]{:S(2)}) collective-permute-start(bf16[1,2,2,2,24,1280]{5,4,3,2,1,0:T(8,128)(2,1)S(1)} %pad_maximum_fusion.15), channel_id=1, source_target_pairs={{0,2},{2,0},{4,6},{6,4},{8,10},{10,8},{12,14},{14,12},{16,18},{18,... | collective-permute-start | bytes 1474568 | tf_op jit(solution)/shard_map/ppermute | solution.py:32
  371.3 40.2 %collective-permute-start.90 = (bf16[1,2,2,2,24,1280]{5,4,3,2,1,0:T(8,128)(2,1)}, bf16[1,2,2,2,24,1280]{5,4,3,2,1,0:T(8,128)(2,1)}, u32[]{:S(2)}, u32[]{:S(2)}) collective-permute-start(bf16[1,2,2,2,24,1280]{5,4,3,2,1,0:T(8,128)(2,1)} %dynamic-slice_convert_fusion), channel_id=1, source_target_pairs={{0,2},{2,0},{4,6},{6,4},{8,10},{10,8},{12,14},{14,12},{16,18},{18,... | collective-permute-start | bytes 1474568 | tf_op jit(solution)/shard_map/ppermute | solution.py:32
  396.5 37.1 %collective-permute-start.80 = (bf16[1,2,2,2,24,1280]{5,4,3,2,1,0:T(8,128)(2,1)S(1)}, bf16[1,2,2,2,24,1280]{5,4,3,2,1,0:T(8,128)(2,1)S(1)}, u32[]{:S(2)}, u32[]{:S(2)}) collective-permute-start(bf16[1,2,2,2,24,1280]{5,4,3,2,1,0:T(8,128)(2,1)S(1)} %dynamic-slice_convert_fusion.1), channel_id=1, source_target_pairs={{0,2},{2,0},{4,6},{6,4},{8,10},{10,8},{12,14},{14,12},{16,18},{18,... | collective-permute-start | bytes 1474568 | tf_op jit(solution)/shard_map/ppermute | solution.py:32
  412.8 10.6 %collective-permute-start.91 = (bf16[1,2,1,1,24,1280]{5,4,3,2,1,0:T(8,128)(2,1)S(1)}, bf16[1,2,1,1,24,1280]{5,4,3,2,1,0:T(8,128)(2,1)S(1)}, u32[]{:S(2)}, u32[]{:S(2)}) collective-permute-start(bf16[1,2,1,1,24,1280]{5,4,3,2,1,0:T(8,128)(2,1)S(1)} %get-tuple-element.98), channel_id=1, source_target_pairs={{0,8},{2,10},{4,12},{6,14},{8,0},{10,2},{12,4},{14,6},{16,24},{18,... | collective-permute-start | bytes 368648 | tf_op jit(solution)/shard_map/ppermute | solution.py:32
  414.1 9.3 %collective-permute-start.93 = (bf16[1,2,1,1,24,1280]{5,4,3,2,1,0:T(8,128)(2,1)S(1)}, bf16[1,2,1,1,24,1280]{5,4,3,2,1,0:T(8,128)(2,1)S(1)}, u32[]{:S(2)}, u32[]{:S(2)}) collective-permute-start(bf16[1,2,1,1,24,1280]{5,4,3,2,1,0:T(8,128)(2,1)S(1)} %get-tuple-element.99), channel_id=1, source_target_pairs={{0,24},{2,26},{4,28},{6,30},{8,16},{10,18},{12,20},{14,22},{16,8},... | collective-permute-start | bytes 368648 | tf_op jit(solution)/shard_map/ppermute | solution.py:32
  416.1 11.6 %collective-permute-start.92 = (bf16[1,2,1,1,24,1280]{5,4,3,2,1,0:T(8,128)(2,1)S(1)}, bf16[1,2,1,1,24,1280]{5,4,3,2,1,0:T(8,128)(2,1)S(1)}, u32[]{:S(2)}, u32[]{:S(2)}) collective-permute-start(bf16[1,2,1,1,24,1280]{5,4,3,2,1,0:T(8,128)(2,1)S(1)} %get-tuple-element.100), channel_id=1, source_target_pairs={{0,16},{2,18},{4,20},{6,22},{8,24},{10,26},{12,28},{14,30},{16,0},... | collective-permute-start | bytes 368648 | tf_op jit(solution)/shard_map/ppermute | solution.py:32
  439.1 12.0 %collective-permute-start.97 = (bf16[1,2,1,1,24,1280]{5,4,3,2,1,0:T(8,128)(2,1)S(1)}, bf16[1,2,1,1,24,1280]{5,4,3,2,1,0:T(8,128)(2,1)S(1)}, u32[]{:S(2)}, u32[]{:S(2)}) collective-permute-start(bf16[1,2,1,1,24,1280]{5,4,3,2,1,0:T(8,128)(2,1)S(1)} %pad_maximum_fusion.52), channel_id=1, source_target_pairs={{0,16},{2,18},{4,20},{6,22},{8,24},{10,26},{12,28},{14,30},{16,0},... | collective-permute-start | bytes 368648 | tf_op jit(solution)/shard_map/ppermute | solution.py:32
  439.1 14.6 %collective-permute-start.96 = (bf16[1,2,1,1,24,1280]{5,4,3,2,1,0:T(8,128)(2,1)S(1)}, bf16[1,2,1,1,24,1280]{5,4,3,2,1,0:T(8,128)(2,1)S(1)}, u32[]{:S(2)}, u32[]{:S(2)}) collective-permute-start(bf16[1,2,1,1,24,1280]{5,4,3,2,1,0:T(8,128)(2,1)S(1)} %pad_maximum_fusion.52), channel_id=1, source_target_pairs={{0,8},{2,10},{4,12},{6,14},{8,0},{10,2},{12,4},{14,6},{16,24},{18,... | collective-permute-start | bytes 368648 | tf_op jit(solution)/shard_map/ppermute | solution.py:32
  441.6 9.6 %collective-permute-start.82 = (bf16[1,1,1,1,24,1280]{5,4,3,2,1,0:T(8,128)(2,1)S(1)}, bf16[1,1,1,1,24,1280]{5,4,3,2,1,0:T(8,128)(2,1)S(1)}, u32[]{:S(2)}, u32[]{:S(2)}) collective-permute-start(bf16[1,1,1,1,24,1280]{5,4,3,2,1,0:T(8,128)(2,1)S(1)} %get-tuple-element.124), channel_id=1, source_target_pairs={{0,8},{2,10},{4,12},{6,14},{8,0},{10,2},{12,4},{14,6},{16,24},{18,... | collective-permute-start | bytes 184328 | tf_op jit(solution)/shard_map/ppermute | solution.py:32
  441.6 9.5 %collective-permute-start.84 = (bf16[1,1,1,1,24,1280]{5,4,3,2,1,0:T(8,128)(2,1)S(1)}, bf16[1,1,1,1,24,1280]{5,4,3,2,1,0:T(8,128)(2,1)S(1)}, u32[]{:S(2)}, u32[]{:S(2)}) collective-permute-start(bf16[1,1,1,1,24,1280]{5,4,3,2,1,0:T(8,128)(2,1)S(1)} %get-tuple-element.125), channel_id=1, source_target_pairs={{0,24},{2,26},{4,28},{6,30},{8,16},{10,18},{12,20},{14,22},{16,8},... | collective-permute-start | bytes 184328 | tf_op jit(solution)/shard_map/ppermute | solution.py:32
  (73 other events, 524.4 us)
